TPU v7x, 128 devices: a whole 4x4x4 slice. The times are simulated.
128 devices in a mesh: grp: 4 (over z_hi, core), mem: 32 (over x, y, z_lo).
Axes of the slice: x: 4, y: 4, z: 4 (z_hi: 2, z_lo: 2; z = z_hi * 2 + z_lo), core: 2. Of those that a mesh axis runs over, the one named last changes fastest.
Arguments:
- perturb: float32 [128, 1024, 1024], P(('grp', 'mem')), may hold values from -0.1875 to 0.1875
- touched_vertex_index: int32 [128, 4, 64], P(('grp', 'mem')), may hold values from 0 to 1023
- proposed_spin_values: int32 [128, 4, 64], P(('grp', 'mem')), may hold values from 0 to 1
- accept: int32 [128, 4, 64], P(('grp', 'mem')), may hold values 0 or 1
- vertex_site_index: int32 [128, 1024], P(('grp', 'mem')), may hold values from 0 to 63
- vertex_time_index: int32 [128, 1024], P(('grp', 'mem')), may hold values from 0 to 4095
- left_proj: float32 [64, 1024], replicated, may hold values from -0.06 to 0.06
- right_proj: float32 [64, 1024], replicated, may hold values from -0.06 to 0.06
- weights: float32 [128], P(('grp', 'mem')), may hold values from 0.3 to 3
- routing: int32 [128, 1], P(('grp', 'mem')), may hold values from 0 to 31; in each aligned block of 32 rows (0 to 31, 32 to 63, ...) at most 2 rows name the same one
- vertex_function_total: float32 [16, 4096, 4096], P('grp', 'mem'), may hold values from -6 to 6
Outputs:
- four_point_out: float32 [16, 4096, 4096], P('grp', 'mem')
Inputs may be any that keep to these rules, and one draw needn't show every extreme that they name: `routing`: among the 32 walkers of one group no member index is named by more than 2 walkers, and in some group one index is named by exactly 2.
All inputs are finite; a program needn't handle non-finite values. No bound on the sum of `accept` on one device may be relied on, other than what follows from the above.
Results may differ from a plain program's by a relative error of at most 0.0003.
Values sent between devices are 32-bit elements; how exact they have to be, the bound alone decides.
No kernel may reach another device: no remote copies, remote signals or barrier semaphores. Data moves between devices by JAX's collectives and lax.ppermute only.
A program may use at most 128 MiB of HBM per device.

v0:
```python
import jax
import jax.numpy as jnp
from jax import lax
from jax.sharding import PartitionSpec as P

K = 1024
SITES = 64
LEG = 64
Q = 16
TIMES = 4096
UPDATES = 4


EXACT_ARITHMETIC = lax.Precision.HIGHEST


def total_of_pieces(shard, axis):
    pieces = lax.all_gather(shard, axis)
    return pieces.sum(axis=0)


def legendre(time_ids):
    abscissa = (2.0 * time_ids.astype(jnp.float32) + 1.0) / TIMES - 1.0
    polys = [jnp.ones_like(abscissa), abscissa]
    for degree in range(1, LEG - 1):
        polys.append(
            ((2 * degree + 1) * abscissa * polys[degree] - degree * polys[degree - 1])
            / (degree + 1)
        )
    norms = jnp.sqrt(2.0 * jnp.arange(LEG, dtype=jnp.float32) + 1.0)
    return jnp.stack(polys[:LEG], axis=1) * norms[None, :]


def make_onehot(site_ids):
    return (site_ids[:, None] == jnp.arange(SITES, dtype=jnp.int32)[None, :]).astype(jnp.float32)


def project(onehot, polys, table):
    spread = jnp.dot(onehot, table, precision=EXACT_ARITHMETIC, preferred_element_type=jnp.float32)
    return jnp.sum(spread.reshape(-1, LEG, Q) * polys[:, :, None], axis=1)


def transform(onehot, polys, values):
    weighted = (polys[:, :, None] * values[:, None, :]).reshape(-1, LEG * Q)
    summed = jnp.dot(
        onehot.T, weighted, precision=EXACT_ARITHMETIC, preferred_element_type=jnp.float32
    )
    return summed.reshape(SITES, LEG, Q).transpose(2, 0, 1).reshape(Q, SITES * LEG)


def update_walker(perturb, touched_vertex_index, proposed_spin_values, accept):
    matrix = jnp.eye(K, dtype=jnp.float32) + perturb
    gammas = accept.astype(jnp.float32) * jnp.where(proposed_spin_values == 1, 0.6, -0.4).astype(
        jnp.float32
    )
    positions = jnp.arange(K, dtype=jnp.int32)

    def apply_update(update, matrix):
        chosen = touched_vertex_index[update]
        unit_cols = (positions[:, None] == chosen[None, :]).astype(jnp.float32)
        columns = (jnp.take(matrix, chosen, axis=1) - unit_cols) * gammas[update][None, :]
        row_block = jnp.take(matrix, chosen, axis=0)
        return matrix - jnp.dot(
            columns, row_block, precision=EXACT_ARITHMETIC, preferred_element_type=jnp.float32
        )

    return lax.fori_loop(0, UPDATES, apply_update, matrix)


def reduce_measured_rows(rescaled_rows, right_observed, vertex_function_total):
    left_q, right_q = (
        lax.all_to_all(rescaled_rows, "grp", split_axis=1, concat_axis=0, tiled=True),
        lax.all_to_all(right_observed, "grp", split_axis=1, concat_axis=0, tiled=True),
    )
    left_rows = lax.all_to_all(left_q, "mem", split_axis=2, concat_axis=0, tiled=True)
    return vertex_function_total + jnp.einsum(
        "mqr,mqc->qrc",
        left_rows,
        lax.all_gather(right_q, "mem", axis=0, tiled=True),
        precision=EXACT_ARITHMETIC,
    )


def per_device(
    perturb,
    touched_vertex_index,
    proposed_spin_values,
    accept,
    vertex_site_index,
    vertex_time_index,
    left_proj,
    right_proj,
    weights,
    routing,
    vertex_function_total,
):
    matrix = update_walker(perturb[0], touched_vertex_index[0], proposed_spin_values[0], accept[0])
    polys = legendre(vertex_time_index[0])
    onehot = make_onehot(vertex_site_index[0])
    left_vec = project(onehot, polys, left_proj)
    right_vec = project(onehot, polys, right_proj)
    left_image = jnp.dot(
        matrix, left_vec, precision=EXACT_ARITHMETIC, preferred_element_type=jnp.float32
    )
    right_image = jnp.dot(
        matrix.T, right_vec, precision=EXACT_ARITHMETIC, preferred_element_type=jnp.float32
    )
    member_mask = (jnp.arange(lax.axis_size("mem"), dtype=jnp.int32) == routing[0, 0]).astype(
        jnp.float32
    )
    totals = total_of_pieces(member_mask * weights[0], "mem")
    own_total = jnp.sum(totals * member_mask)
    gamma_factor_list = weights / own_total
    left_observed = transform(onehot, polys, left_image)[None]
    right_observed = transform(onehot, polys, right_image)[None]
    rescaled_rows = left_observed * gamma_factor_list[:, None, None]
    return reduce_measured_rows(rescaled_rows, right_observed, vertex_function_total)


def solution(mesh):
    in_specs = (
        P(("grp", "mem"), None, None),
        P(("grp", "mem"), None, None),
        P(("grp", "mem"), None, None),
        P(("grp", "mem"), None, None),
        P(("grp", "mem"), None),
        P(("grp", "mem"), None),
        P(),
        P(),
        P(("grp", "mem")),
        P(("grp", "mem"), None),
        P("grp", "mem", None),
    )
    out_specs = P("grp", "mem", None)
    return jax.shard_map(
        per_device, mesh=mesh, in_specs=in_specs, out_specs=out_specs, check_vma=False
    )
```

profile of v0, /device:TPU:0, one launch (start us, length us, event | category | flops | bytes accessed | tf_op | source)
XLA Modules:
  0.0 348.2 jit_solution(41468833753186495)
XLA Ops:
  6.5 0.0 copy-start
  6.5 0.0 all-gather.3.cloned.1.call-start
  6.6 1.1 subtract_multiply_fusion.2
  7.7 0.2 subtract_multiply_fusion
  7.9 0.0 copy-done
  7.9 0.0 copy-start.3
  7.9 4.7 %fusion.34 = f32[1024,1024]{0,1:T(8,128)} fusion(f32[64,1024]{1,0:T(8,128)S(1)} %copy-done, s32[1024]{0:T(1024)} %bitcast.186), kind=kOutput, calls=%fused_computation.42 | convolution fusion | flops 805371904 | bytes 4460544 | tf_op jit(solution)/shard_map/dot_general | solution.py:39
  12.6 0.0 copy-done.5
  12.6 0.0 copy-done.4
  12.6 3.8 %fusion.32 = f32[1024,1024]{0,1:T(8,128)} fusion(f32[64,1024]{1,0:T(8,128)S(1)} %copy-done.4, s32[1024]{0:T(1024)S(1)} %bitcast.187), kind=kOutput, calls=%fused_computation.40 | convolution fusion | flops 805371904 | bytes 4460544 | tf_op jit(solution)/shard_map/dot_general | solution.py:39
  16.4 0.0 copy-done.3
  16.4 2.4 bitcast_add_fusion
  18.8 0.0 copy-done.7
  18.8 0.0 copy-done.8
  18.8 0.0 copy-done.6
  18.8 72.9 %while.14 = (s32[]{:T(128)}, f32[1024,1024]{1,0:T(8,128)}, s32[4,64]{1,0:T(4,128)S(1)}, f32[4,64]{1,0:T(4,128)S(1)}, s32[]{:T(128)}) while((s32[]{:T(128)}, f32[1024,1024]{1,0:T(8,128)}, s32[4,64]{1,0:T(4,128)S(1)}, f32[4,64]{1,0:T(4,128)S(1)}, s32[]{:T(128)}) %tuple.131), condition=%wide.region_1.2_spmd.clone, body=%wide.region_0.1_spmd.clone.sunk | while | flops 806749760 | bytes 18357192 | solution.py:67
  18.9 5.4 %copy.48 = f32[1024,1024]{0,1:T(8,128)} copy(f32[1024,1024]{1,0:T(8,128)} %get-tuple-element.275) | data formatting | bytes 8388608 | tf_op jit(solution)/shard_map/while
  24.2 3.0 gather_fusion
  27.2 3.0 gather_fusion.1
  30.3 6.8 %convolution_subtract_fusion.2 = f32[1024,1024]{1,0:T(8,128)} fusion(f32[1024,1024]{1,0:T(8,128)} %get-tuple-element.275, f32[64,1024]{1,0:T(8,128)S(1)} %gather_fusion, f32[64,1024]{1,0:T(8,128)S(1)} %gather_fusion.1, f32[64]{0:T(128)S(1)} %dynamic-slice_bitcast_fusion.2, s32[64]{0:T(128)S(1)} %get-tuple-element.267, ...), kind=kOutput, calls=%fused_computation.3.clone.1 | convolution fusion | flops 806748160 | bytes 8913472 | tf_op jit(solution)/shard_map/while/body/eval_jaxpr/dot_general | solution.py:63
  37.1 5.4 %copy.48 = f32[1024,1024]{0,1:T(8,128)} copy(f32[1024,1024]{1,0:T(8,128)} %get-tuple-element.275) | data formatting | bytes 8388608 | tf_op jit(solution)/shard_map/while
  42.4 3.0 gather_fusion
  45.4 3.0 gather_fusion.1
  48.5 6.8 %convolution_subtract_fusion.2 = f32[1024,1024]{1,0:T(8,128)} fusion(f32[1024,1024]{1,0:T(8,128)} %get-tuple-element.275, f32[64,1024]{1,0:T(8,128)S(1)} %gather_fusion, f32[64,1024]{1,0:T(8,128)S(1)} %gather_fusion.1, f32[64]{0:T(128)S(1)} %dynamic-slice_bitcast_fusion.2, s32[64]{0:T(128)S(1)} %get-tuple-element.267, ...), kind=kOutput, calls=%fused_computation.3.clone.1 | convolution fusion | flops 806748160 | bytes 8913472 | tf_op jit(solution)/shard_map/while/body/eval_jaxpr/dot_general | solution.py:63
  55.3 5.4 %copy.48 = f32[1024,1024]{0,1:T(8,128)} copy(f32[1024,1024]{1,0:T(8,128)} %get-tuple-element.275) | data formatting | bytes 8388608 | tf_op jit(solution)/shard_map/while
  60.6 3.0 gather_fusion
  63.6 3.0 gather_fusion.1
  66.6 6.8 %convolution_subtract_fusion.2 = f32[1024,1024]{1,0:T(8,128)} fusion(f32[1024,1024]{1,0:T(8,128)} %get-tuple-element.275, f32[64,1024]{1,0:T(8,128)S(1)} %gather_fusion, f32[64,1024]{1,0:T(8,128)S(1)} %gather_fusion.1, f32[64]{0:T(128)S(1)} %dynamic-slice_bitcast_fusion.2, s32[64]{0:T(128)S(1)} %get-tuple-element.267, ...), kind=kOutput, calls=%fused_computation.3.clone.1 | convolution fusion | flops 806748160 | bytes 8913472 | tf_op jit(solution)/shard_map/while/body/eval_jaxpr/dot_general | solution.py:63
  73.4 5.4 %copy.48 = f32[1024,1024]{0,1:T(8,128)} copy(f32[1024,1024]{1,0:T(8,128)} %get-tuple-element.275) | data formatting | bytes 8388608 | tf_op jit(solution)/shard_map/while
  78.8 3.0 gather_fusion
  81.8 3.0 gather_fusion.1
  84.8 6.8 %convolution_subtract_fusion.2 = f32[1024,1024]{1,0:T(8,128)} fusion(f32[1024,1024]{1,0:T(8,128)} %get-tuple-element.275, f32[64,1024]{1,0:T(8,128)S(1)} %gather_fusion, f32[64,1024]{1,0:T(8,128)S(1)} %gather_fusion.1, f32[64]{0:T(128)S(1)} %dynamic-slice_bitcast_fusion.2, s32[64]{0:T(128)S(1)} %get-tuple-element.267, ...), kind=kOutput, calls=%fused_computation.3.clone.1 | convolution fusion | flops 806748160 | bytes 8913472 | tf_op jit(solution)/shard_map/while/body/eval_jaxpr/dot_general | solution.py:63
  92.2 0.5 stack.62
  92.7 0.1 broadcast_multiply_fusion
  92.8 0.0 copy-start.2
  92.8 4.7 %multiply_reduce_fusion = (f32[1024,16]{0,1:T(8,128)S(1)}, f32[1024,16]{0,1:T(8,128)S(1)}) fusion(f32[1024,64,16]{0,2,1:T(8,128)} %bitcast.180, f32[1024,64]{0,1:T(8,128)S(1)} %broadcast_multiply_fusion, f32[1024,64,16]{0,2,1:T(8,128)} %bitcast.179), kind=kLoop, calls=%fused_computation.32 | loop fusion | flops 4161536 | bytes 8781824 | tf_op jit(solution)/shard_map/reduce_sum | solution.py:40
  97.5 0.0 copy-done.2
  97.5 3.6 %fusion.46 = f32[1024,16]{0,1:T(8,128)S(1)} fusion(f32[1024,1024]{1,0:T(8,128)S(1)} %copy-done.2, f32[1024,16]{0,1:T(8,128)S(1)} %get-tuple-element.111), kind=kOutput, calls=%fused_computation.219 | convolution fusion | flops 201326592 | bytes 4325376 | tf_op jit(solution)/shard_map/dot_general | solution.py:102
  101.1 2.3 fusion.47
  103.4 2.6 multiply_bitcast_fusion
  106.0 5.6 %fusion.23 = f32[16,64,64]{2,1,0:T(8,128)S(1)} fusion(f32[64,16,1024]{2,1,0:T(8,128)S(1)} %get-tuple-element.173, s32[1024]{0:T(1024)S(1)} %bitcast.188), kind=kOutput, calls=%fused_computation.36 | convolution fusion | flops 805371904 | bytes 4460544 | tf_op jit(solution)/shard_map/dot_general | solution.py:45
  111.7 0.3 broadcast_in_dim_reshape.5
  112.0 12.6 %all_to_all.42 = f32[1,16,4096]{2,0,1:T(1,128)S(1)} all-to-all(f32[1,16,4096]{2,0,1:T(1,128)S(1)} %broadcast_in_dim_reshape.5), channel_id=1, replica_groups=mesh['grp'=4,'mem'=32] {'grp'}, dimensions={1} | all-to-all | bytes 524288 | tf_op jit(solution)/shard_map/all_to_all | solution.py:73
  124.6 0.6 reduce.2
  125.2 0.8 all_to_all.38
  126.0 0.0 all-gather.3.cloned.1.call-update
  127.3 81.6 %all-gather = f32[32,1,32]{2,1,0:T(1,128)S(1)} all-gather(f32[1,1,32]{2,1,0:T(1,128)S(1)} %fusion.44), channel_id=1, replica_groups=mesh['grp'=4,'mem'=32] {'mem'}, dimensions={0}, use_global_device_ids=true | all-gather | bytes 4224 | tf_op jit(solution)/shard_map/all_gather | solution.py:18
  208.9 0.1 reduce_sum.37
  209.0 0.6 fusion.43
  210.3 7.4 %fusion.29 = f32[16,64,64]{2,1,0:T(8,128)S(1)} fusion(f32[64,16,1024]{2,1,0:T(8,128)} %get-tuple-element.174, f32[]{:T(128)} %bitcast.35, s32[1024]{0:T(1024)S(1)} %bitcast.189), kind=kOutput, calls=%fused_computation.38 | convolution fusion | flops 805437440 | bytes 4460548 | tf_op jit(solution)/shard_map/dot_general | solution.py:45
  217.7 0.3 mul.18371
  218.0 15.0 %all_to_all.43 = f32[1,16,4096]{2,0,1:T(1,128)S(1)} all-to-all(f32[1,16,4096]{2,0,1:T(1,128)S(1)} %mul.18371), channel_id=1, replica_groups=mesh['grp'=4,'mem'=32] {'grp'}, dimensions={1} | all-to-all | bytes 524288 | tf_op jit(solution)/shard_map/all_to_all | solution.py:72
  233.0 0.6 reduce.1
  233.7 0.1 all_to_all.32
  233.7 5.8 %copy.22 = f32[4,4,4096]{1,0,2:T(4,128)} copy(f32[4,4,4096]{2,1,0:T(4,128)S(1)} %all_to_all.32) | data formatting | bytes 524288 | tf_op jit(solution)/shard_map/all_to_all | solution.py:72
  239.6 11.3 %reshape.1447 = f32[32,1,2048]{2,1,0:T(1,128)S(1)} reshape(f32[4096,4,4]{2,1,0:T(4,128)} %bitcast.177) | data formatting | bytes 524288
  250.9 13.0 %all_to_all.44 = f32[32,1,2048]{2,1,0:T(1,128)S(1)} all-to-all(f32[32,1,2048]{2,1,0:T(1,128)S(1)} %reshape.1447), channel_id=1, replica_groups=mesh['grp'=4,'mem'=32] {'mem'}, dimensions={0} | all-to-all | bytes 524288 | tf_op jit(solution)/shard_map/all_to_all | solution.py:75
  263.9 0.5 broadcast.19334
  264.4 1.3 reduce.3
  265.7 12.2 %reshape.1448 = f32[4096,4,4]{2,1,0:T(4,128)} reshape(f32[32,2048]{1,0:T(8,128)S(1)} %reduce.3) | data formatting | bytes 524288
  277.9 5.3 %copy.30 = f32[4,4,32,128]{3,2,1,0:T(8,128)S(1)} copy(f32[4,4,32,128]{1,0,3,2:T(4,128)} %bitcast.178) | data formatting | bytes 524288 | tf_op jit(solution)/shard_map/all_to_all | solution.py:75
  283.2 0.2 copy.24
  283.4 38.9 %all-gather.3.cloned.1.call-done = f32[128,4,4096]{2,1,0:T(4,128)} async-done(((f32[4,4,4096]{2,1,0:T(4,128)}), f32[128,4,4096]{2,1,0:T(4,128)}) %all-gather.3.cloned.1.call-update) | async-done | bytes 8388624 | tf_op jit(solution)/shard_map/all_gather | solution.py:79
  322.3 18.6 %fusion.16 = f32[4,128,4096]{2,1,0:T(8,128)} fusion(f32[4,128,4096]{2,1,0:T(8,128)} %param.23, f32[128,4,128]{2,0,1:T(8,128)S(1)} %bitcast.181, f32[128,4,4096]{2,1,0:T(4,128)} %all-gather.3.cloned.1.call-done), kind=kOutput, calls=%fused_computation.25 | convolution fusion | flops 3223322624 | bytes 25427968 | tf_op jit(solution)/shard_map/mqr,mqc->qrc/dot_general | solution.py:76
  (48 shorter events, 0.5 us)
Async XLA Ops:
  6.5 1.4 copy-start
  6.5 6.1 %copy-start.5 = (s32[1,1024]{1,0:T(1,128)S(1)}, s32[1,1024]{1,0:T(1,128)}, u32[]{:S(2)}) copy-start(s32[1,1024]{1,0:T(1,128)} %param.17) | copy-start | bytes 12292
  6.5 6.1 %copy-start.4 = (f32[64,1024]{1,0:T(8,128)S(1)}, f32[64,1024]{1,0:T(8,128)}, u32[]{:S(2)}) copy-start(f32[64,1024]{1,0:T(8,128)} %param.20) | copy-start | bytes 786436
  6.5 315.7 %all-gather.3.cloned.1.call-start = ((), (), s32[]{:S(2)}) async-start(), calls=%async_computation.3 | async-start | bytes 8650752 | tf_op jit(solution)/shard_map/all_gather | solution.py:79
  7.9 8.5 %copy-start.3 = (f32[1,1024,1024]{2,1,0:T(8,128)S(1)}, f32[1,1024,1024]{2,1,0:T(8,128)}, u32[]{:S(2)}) copy-start(f32[1,1024,1024]{2,1,0:T(8,128)} %param.13) | copy-start | bytes 12582916
  16.4 2.4 copy-start.7
  16.4 2.4 copy-start.8
  16.4 2.4 copy-start.6
  92.8 4.7 %copy-start.2 = (f32[1024,1024]{1,0:T(8,128)S(1)}, f32[1024,1024]{1,0:T(8,128)}, u32[]{:S(2)}) copy-start(f32[1024,1024]{1,0:T(8,128)} %get-tuple-element.99) | copy-start | bytes 12582916
  322.3 18.6 %copy-start.1 = (f32[64,1024]{1,0:T(8,128)S(1)}, f32[64,1024]{1,0:T(8,128)}, u32[]{:S(2)}) copy-start(f32[64,1024]{1,0:T(8,128)} %param.19) | copy-start | bytes 786436
Sparse Core Ops, SparseCore 0:
  126.1 196.1 all-gather.2
where the time goes:
time: 355 us; the launch traced here: 348 us
  blocking collectives  122 us (34%)
  local copies, waits for them, and re-layouts  82.8 us (23%)
  matrix products  73.2 us (21%)
  waiting for transfers between devices  38.9 us (11%)
  between operations  16.1 us (5%)
  other arithmetic  14.7 us (4%)
    all_gather x1, blocking collectives, total_of_pieces(): pieces = lax.all_gather(shard, axis)  81.6 us
    all_gather x1, waiting for transfers between devices, reduce_measured_rows(): lax.all_gather(right_q, 'mem', axis=0, tiled=True)  38.9 us
    dot_general x4, matrix products, apply_update(): jnp.dot(columns, row_block, precision=EXACT_ARITHMETIC, preferred_element...  27.2 us
    unnamed x20, local copies, waits for them, and re-layouts  23.6 us
    while x4, local copies, waits for them, and re-layouts  21.5 us
    dot_general x1, matrix products, reduce_measured_rows(): jnp.einsum('mqr,mqc->qrc', left_rows, lax.all_gather(right_q, 'mem', axis...  18.6 us
    all_to_all x1, blocking collectives, reduce_measured_rows(): lax.all_to_all(rescaled_rows, 'grp', split_axis=1, concat_axis=0, tiled=T...  15 us
    dot_general x2, matrix products, transform(): jnp.dot(onehot.T, weighted, precision=EXACT_ARITHMETIC, preferred_element...  13 us
  transfers between devices with their start and end apart: 1, of which 1 were waited for; matrix products, arithmetic and copies ran while one was open for 13% of the time, Pallas kernels for 0%

commit v1 on v0

v1 whole, which is shorter than its diff:
```python
import functools

import jax
import jax.numpy as jnp
import numpy as np
from jax import lax
from jax.experimental import pallas as pl
from jax.experimental.pallas import tpu as pltpu
from jax.sharding import Mesh
from jax.sharding import PartitionSpec as P

K = 1024
SITES = 64
LEG = 64
Q = 16
TIMES = 4096
UPDATES = 4
RANKB = 64
NS = UPDATES * RANKB
GQ = 4
RIGHT_ROWS = GQ * 32
LEFT_ROWS = GQ * 16
BLOCK_ROWS = RIGHT_ROWS + LEFT_ROWS + 8
PIECE_ROWS = 4 * RIGHT_ROWS + 8
F32 = jnp.float32
BF16 = jnp.bfloat16
NN = (((1,), (0,)), ((), ()))
NT = (((1,), (1,)), ((), ()))
TN = (((0,), (0,)), ((), ()))
MIB = 1 << 20


def mm(a, b, dims=NN):
    return lax.dot_general(a, b, dims, preferred_element_type=F32)


def split2(x):
    hi = x.astype(BF16)
    return hi, (x - hi.astype(F32)).astype(BF16)


def split3(x):
    hi = x.astype(BF16)
    rest = x - hi.astype(F32)
    mid = rest.astype(BF16)
    return hi, mid, (rest - mid.astype(F32)).astype(BF16)


def mm3(a, b, dims=NN):
    ah, al = a if isinstance(a, tuple) else split2(a)
    bh, bl = b if isinstance(b, tuple) else split2(b)
    return mm(ah, bh, dims) + (mm(al, bh, dims) + mm(ah, bl, dims))


def iota(shape, dim):
    return lax.broadcasted_iota(jnp.int32, shape, dim)


def row_to_column(row):
    n = row.shape[1]
    same = iota((n, n), 0) == iota((n, n), 1)
    return jnp.sum(jnp.where(same, row, jnp.zeros_like(row)), axis=1, keepdims=True)


def measure_kernel(
    place_ref, chosen_ref, gamma_ref, site_ref, time_ref, left_ref, right_ref, weight_ref, key_ref, perturb_ref,
    *rest,
):
    outs = rest[:8]
    (matrix, p_hi, p_lo, polys, spread, vecs, left_meas, right_meas, sem) = rest[8:]
    load = pltpu.make_async_copy(perturb_ref.at[0], matrix, sem)
    load.start()

    abscissa = (2.0 * time_ref[...].astype(F32) + 1.0) / TIMES - 1.0
    before, now = jnp.ones_like(abscissa), abscissa
    polys[0:1, :] = before
    polys[1:2, :] = now * float(np.sqrt(3.0))
    for degree in range(1, LEG - 1):
        after = abscissa * now * ((2 * degree + 1) / (degree + 1)) - before * (degree / (degree + 1))
        before, now = now, after
        polys[degree + 1 : degree + 2, :] = now * float(np.sqrt(2.0 * degree + 3.0))

    sites = site_ref[...]
    onehot = (iota((SITES, K), 0) == sites).astype(F32).astype(BF16)
    onehot3 = jnp.concatenate([onehot, onehot, onehot], axis=0)
    for side, table_ref in ((0, left_ref), (1, right_ref)):
        table = jnp.concatenate(split3(table_ref[...]), axis=0)
        spread[...] = mm(table, onehot3, TN)
        total = jnp.zeros((Q, K), F32)
        for degree in range(LEG):
            total = total + spread[degree * Q : (degree + 1) * Q, :] * polys[degree : degree + 1, :]
        vecs[side] = total

    chosen = row_to_column(chosen_ref[...].astype(F32)).astype(jnp.int32)
    pick = (iota((NS, K), 1) == chosen).astype(F32).astype(BF16)
    gamma = gamma_ref[...]
    load.wait()
    for step in range(4):
        rows = slice(step * 256, (step + 1) * 256)
        hi, lo = split2(matrix[rows, :])
        p_hi[rows, :] = hi
        p_lo[rows, :] = lo
    ph, plo = p_hi[...], p_lo[...]
    v, w = vecs[0], vecs[1]
    wh, wl = split2(w)
    high = mm(jnp.concatenate([pick, wh, wl], axis=0), ph)
    low = mm(jnp.concatenate([pick, wh], axis=0), plo)
    rows_hi, rows_lo = high[:NS].astype(BF16), low[:NS].astype(BF16)
    from_w = high[NS : NS + Q] + high[NS + Q :] + low[NS:]
    same = mm(pick, pick, NT)
    small = mm(rows_hi, pick, NT) + mm(rows_lo, pick, NT)
    vs = split3(v)
    p_vec = (mm(vs[0], pick, NT) + mm(vs[1], pick, NT) + mm(vs[2], pick, NT)) + mm3(
        (vs[0], vs[1]), (rows_hi, rows_lo), NT
    )
    fs = split3(from_w)
    q_vec = mm(fs[0], pick, NT) + mm(fs[1], pick, NT) + mm(fs[2], pick, NT)
    row_block = lax.div(iota((NS, NS), 0), RANKB)
    col_block = lax.div(iota((NS, NS), 1), RANKB)
    c_all, r_all = jnp.zeros((NS, NS), F32), jnp.zeros((NS, NS), F32)
    for update in range(UPDATES):
        columns = jnp.where(col_block == update, small * gamma, 0.0)
        rows_now = small + same
        c_all = c_all + columns
        r_all = jnp.where(row_block == update, rows_now, r_all)
        if update < UPDATES - 1:
            small = small - mm3(columns, rows_now)
    lower = split2(jnp.where(row_block > col_block, c_all, 0.0))
    upper = split2(jnp.where(row_block < col_block, r_all, 0.0))
    x, y = p_vec, q_vec * gamma
    for _ in range(UPDATES - 1):
        x = p_vec - mm3(x, lower, NT)
        y = (q_vec - mm3(y, upper)) * gamma
    z, y2 = x, y
    for _ in range(UPDATES - 1):
        z = x - mm3(z * gamma, upper, NT)
        y2 = y - mm3(y2, lower)
    zs, ys = split3(z * gamma), split3(y2)
    left_arg = v - (mm(zs[0], pick) + mm(zs[1], pick) + mm(zs[2], pick))
    left_image = v + mm3(left_arg, (ph, plo), NT)
    right_arg = w - (mm(ys[0], pick) + mm(ys[1], pick) + mm(ys[2], pick))
    right_image = right_arg + from_w - mm3((ys[0], ys[1]), (rows_hi, rows_lo))

    pol_hi, pol_lo = split2(polys[...])
    both = jnp.concatenate([pol_hi, pol_hi, pol_lo, pol_lo], axis=0)
    even_site = iota((32, K), 0) * 2 == sites
    odd_site = iota((32, K), 0) * 2 + 1 == sites
    first_lanes = iota((64, 128), 1) < LEG
    for image, meas in ((right_image, right_meas), (left_image, left_meas)):
        ih = image.astype(BF16).astype(F32)
        il = image - ih
        for q in range(0, Q, 2):
            def masked(site, part):
                return jnp.concatenate(
                    [jnp.where(site, part[q + k : q + k + 1, :], 0.0).astype(BF16) for k in range(2)], axis=0
                )
            tops = jnp.concatenate([masked(even_site, ih), masked(odd_site, ih)], axis=0)
            bots = jnp.concatenate([masked(even_site, il), masked(odd_site, il)], axis=0)
            high = mm(tops, both, NT)
            low = mm(bots, both[:128], NT)
            whole = high[:, :128] + (high[:, 128:] + low)
            meas[q * 32 : (q + 2) * 32, :] = jnp.where(first_lanes, whole[:64], whole[64:])

    lane = iota((8, 128), 1)
    meta = jnp.where(lane == 0, weight_ref[0], jnp.where(lane == 1, key_ref[0], 0.0))
    for distance in range(8):
        target = place_ref[0] ^ distance
        group, half = target // 2, target % 2
        first = pl.multiple_of(group * RIGHT_ROWS, RIGHT_ROWS)
        outs[distance][0:RIGHT_ROWS, :] = right_meas[pl.ds(first, RIGHT_ROWS), :]
        outs[distance][RIGHT_ROWS : RIGHT_ROWS + LEFT_ROWS, :] = left_meas[pl.ds(first + half, LEFT_ROWS, stride=2), :]
        outs[distance][RIGHT_ROWS + LEFT_ROWS :, :] = meta


def assemble_kernel(place_ref, *refs):
    blocks, pieces, lefts = refs[:8], refs[8:10], refs[10:]
    for d in range(8):
        pieces[d // 4][(d % 4) * RIGHT_ROWS : (d % 4 + 1) * RIGHT_ROWS, :] = blocks[d][0:RIGHT_ROWS, :]
    for half in range(2):
        pieces[half][4 * RIGHT_ROWS :, :] = jnp.concatenate(
            [blocks[half * 4 + d][RIGHT_ROWS + LEFT_ROWS : RIGHT_ROWS + LEFT_ROWS + 2, :] for d in range(4)], axis=0
        )
    for dx in range(4):
        for dy in range(4):
            owner = ((place_ref[0] + dx) % 4) * 4 + (place_ref[1] + dy) % 4
            for d in range(8):
                row = (dy * 8 + d) * GQ
                lefts[dx][row : row + GQ, :] = blocks[d][pl.ds(RIGHT_ROWS + owner, GQ, stride=16), :]


CHUNK = 8


def final_kernel(*refs):
    lefts, pieces, total_ref = refs[:4], refs[4:36], refs[36]
    out_ref, rows, meta, factors, l_top, sem = refs[37:]
    step = pl.program_id(0) * pl.num_programs(1) + pl.program_id(1)

    @pl.when(step == 0)
    def _():
        copies = []
        for i, piece in enumerate(pieces):
            place, colour = i // 2, i % 2
            copies.append(
                pltpu.make_async_copy(
                    piece.at[pl.ds(0, 4 * RIGHT_ROWS)],
                    rows.at[pl.ds((place * 8 + colour * 4) * RIGHT_ROWS, 4 * RIGHT_ROWS)],
                    sem.at[0],
                )
            )
            copies.append(
                pltpu.make_async_copy(
                    piece.at[pl.ds(4 * RIGHT_ROWS, 8)],
                    meta.at[pl.ds((place * 2 + colour) * 8, 8)],
                    sem.at[0],
                )
            )
        for copy in copies:
            copy.start()
        for copy in copies:
            copy.wait()
        mine = meta[pl.ds(0, 128, stride=2), :]
        weight, key = mine[:, 0:1], mine[:, 1:2]
        diag = iota((128, 128), 0) == iota((128, 128), 1)
        key_row = jnp.sum(jnp.where(diag, key, 0.0), axis=0, keepdims=True)
        weight_row = jnp.sum(jnp.where(diag, weight, 0.0), axis=0, keepdims=True)
        own = jnp.sum(jnp.where(key == key_row, weight_row, 0.0), axis=1, keepdims=True)
        factors[...] = jnp.broadcast_to(weight / own, (128, 128))

    q = pl.program_id(0)

    @pl.when(pl.program_id(1) == 0)
    def _():
        left = jnp.concatenate([lefts[sy][pl.ds(q, 32, stride=GQ), :] for sy in range(4)], axis=0)
        hi, lo = split2(left * factors[...])
        l_top[...] = jnp.concatenate([hi, lo, hi], axis=0)

    left3 = l_top[...]
    for j in range(CHUNK):
        first = q * 32 + pl.program_id(1) * CHUNK + j
        hi, lo = split2(rows[pl.ds(first, 128, stride=RIGHT_ROWS), :])
        right3 = jnp.concatenate([hi, hi, lo], axis=0)
        cols = slice(j * 128, (j + 1) * 128)
        out_ref[0, :, cols] = total_ref[0, :, cols] + mm(left3, right3, TN)


ANY = pl.BlockSpec(memory_space=pl.ANY)
VMEM = pl.BlockSpec(memory_space=pltpu.VMEM)
SMEM = pl.BlockSpec(memory_space=pltpu.SMEM)


def sds(*shape):
    return jax.ShapeDtypeStruct(shape, F32)


def gather_plane(piece, first, second):
    up = [(i, (i + 1) % 4) for i in range(4)]
    down = [(i, (i - 1) % 4) for i in range(4)]
    line = {0: piece, 3: lax.ppermute(piece, first, up), 1: lax.ppermute(piece, first, down)}
    line[2] = lax.ppermute(line[3], first, up)
    found = {}
    for a in range(4):
        found[a, 0] = line[a]
        found[a, 3] = lax.ppermute(line[a], second, up)
        found[a, 1] = lax.ppermute(line[a], second, down)
        found[a, 2] = lax.ppermute(found[a, 3], second, up) if a % 2 == 0 else lax.ppermute(found[a, 1], second, down)
    return found if first == "x" else {(b, a): value for (a, b), value in found.items()}


def per_device(perturb, touched, spins, accept, site_ids, time_ids, left_proj, right_proj, weights, routing, total):
    column = lax.axis_index(("zh", "c", "zl"))
    group = lax.axis_index(("zh", "c"))
    chosen = touched.reshape(1, NS)
    gamma = (accept.astype(F32) * jnp.where(spins == 1, 0.6, -0.4).astype(F32)).reshape(1, NS)
    key = (routing[0] + 32 * group).astype(F32)
    blocks = pl.pallas_call(
        measure_kernel,
        out_shape=[sds(BLOCK_ROWS, 128)] * 8,
        in_specs=[SMEM] + [VMEM] * 6 + [SMEM, SMEM, ANY],
        out_specs=[VMEM] * 8,
        scratch_shapes=[
            pltpu.VMEM((K, K), F32),
            pltpu.VMEM((K, K), BF16),
            pltpu.VMEM((K, K), BF16),
            pltpu.VMEM((LEG, K), F32),
            pltpu.VMEM((LEG * Q, K), F32),
            pltpu.VMEM((2, Q, K), F32),
            pltpu.VMEM((Q * 32, 128), F32),
            pltpu.VMEM((Q * 32, 128), F32),
            pltpu.SemaphoreType.DMA,
        ],
        compiler_params=pltpu.CompilerParams(vmem_limit_bytes=56 * MIB),
        name="measure",
    )(column[None], chosen, gamma, site_ids, time_ids, left_proj, right_proj, weights, key, perturb)
    here = [blocks[0]] + [
        lax.ppermute(blocks[d], ("zh", "c", "zl"), [(i, i ^ d) for i in range(8)]) for d in range(1, 8)
    ]
    plane = jnp.stack([lax.axis_index("x"), lax.axis_index("y")]).astype(jnp.int32)
    first, second, *lefts = pl.pallas_call(
        assemble_kernel,
        out_shape=[sds(PIECE_ROWS, 128)] * 2 + [sds(128, 128)] * 4,
        in_specs=[SMEM] + [VMEM] * 8,
        out_specs=[VMEM] * 6,
        name="assemble",
    )(plane, *here)
    one, two = gather_plane(first, "x", "y"), gather_plane(second, "y", "x")
    from_x = {0: lefts[0]}
    for dx in range(1, 4):
        from_x[4 - dx] = lax.ppermute(lefts[dx], "x", [(i, (i + dx) % 4) for i in range(4)])
    rows_of = [jnp.concatenate([from_x[sx][dy * 32 : (dy + 1) * 32] for sx in range(4)], axis=0) for dy in range(4)]
    from_y = {0: rows_of[0]}
    for dy in range(1, 4):
        from_y[4 - dy] = lax.ppermute(rows_of[dy], "y", [(i, (i + dy) % 4) for i in range(4)])
    pieces = []
    for sy in range(4):
        for sx in range(4):
            pieces += [one[sx, sy], two[sx, sy]]
    block = pl.BlockSpec((1, 128, CHUNK * 128), lambda q, n: (q, 0, n))
    return pl.pallas_call(
        final_kernel,
        grid=(GQ, 32 // CHUNK),
        out_shape=sds(GQ, 128, SITES * LEG),
        in_specs=[VMEM] * 4 + [ANY] * 32 + [block],
        out_specs=block,
        scratch_shapes=[
            pltpu.VMEM((128 * RIGHT_ROWS, 128), F32),
            pltpu.VMEM((256, 128), F32),
            pltpu.VMEM((128, 128), F32),
            pltpu.VMEM((384, 128), BF16),
            pltpu.SemaphoreType.DMA((1,)),
        ],
        compiler_params=pltpu.CompilerParams(vmem_limit_bytes=40 * MIB),
        name="accumulate",
    )(*[from_y[sy] for sy in range(4)], *pieces, total)


def solution(mesh):
    cube = Mesh(mesh.devices.reshape(2, 2, 4, 4, 2), ("zh", "c", "x", "y", "zl"))
    grp, mem = ("zh", "c"), ("x", "y", "zl")
    both = grp + mem
    in_specs = (
        P(both, None, None),
        P(both, None, None),
        P(both, None, None),
        P(both, None, None),
        P(both, None),
        P(both, None),
        P(),
        P(),
        P(both),
        P(both, None),
        P(grp, mem, None),
    )
    return jax.shard_map(per_device, mesh=cube, in_specs=in_specs, out_specs=P(grp, mem, None), check_vma=False)
```

time: 355 us -> 145 us (0.41); the launches traced: 348 us -> 144 us
  blocking collectives: 122 us -> 0 us
  local copies, waits for them, and re-layouts: 82.8 us -> 5.29 us
  matrix products: 73.2 us -> 0 us
  starting transfers between devices: 0.01 us -> 48.9 us
  Pallas kernels: 0 us -> 35.8 us
  between operations: 16.1 us -> 1.57 us
  other arithmetic: 14.7 us -> 1.3 us
  waiting for transfers between devices: 38.9 us -> 50.8 us
    all_gather x1 -> x0, blocking collectives: 81.6 us -> none  [total_of_pieces(): pieces = lax.all_gather(shard, axis)]
    dot_general x11 -> x0, matrix products: 73.2 us -> none  [the longest x4 27.2 us: apply_update(): jnp.dot(columns, row_block, precision=EXACT_ARITHMETIC, preferred_element...]
    ppermute x0 -> x43, waiting for transfers between devices: none -> 50.8 us  [the longest x8 16.6 us: gather_plane(): found[a, 3] = lax.ppermute(line[a], second, up)]
    ppermute x0 -> x43, starting transfers between devices: none -> 48.9 us  [the longest x8 19.6 us: gather_plane(): found[a, 1] = lax.ppermute(line[a], second, down)]
    all_to_all x3 -> x0, blocking collectives: 40.6 us -> none  [the longest x1 15 us: reduce_measured_rows(): lax.all_to_all(rescaled_rows, 'grp', split_axis=1, concat_axis=0, tiled=T...]
    all_gather x1 -> x0, waiting for transfers between devices: 38.9 us -> none  [reduce_measured_rows(): lax.all_gather(right_q, 'mem', axis=0, tiled=True)]
    pallas_call x0 -> x3, Pallas kernels: none -> 35.8 us  [the longest x1 18.6 us: per_device(): pl.pallas_call(final_kernel, grid=(GQ, 32 // CHUNK), out_shape=sds(GQ, 12...]
    gather x8 -> x0, local copies, waits for them, and re-layouts: 23.9 us -> none  [the longest x4 11.9 us: apply_update(): row_block = jnp.take(matrix, chosen, axis=0)]
  transfers between devices with their start and end apart: 1 -> 43, of which waited for: 1 -> 19; matrix products, arithmetic and copies ran while one was open for 13% -> 1% of each run, Pallas kernels for 0% -> 0%
where the time goes in v1:
time: 145 us; the launch traced here: 144 us
  waiting for transfers between devices  50.8 us (35%)
  starting transfers between devices  48.9 us (34%)
  Pallas kernels  35.8 us (25%)
  local copies, waits for them, and re-layouts  5.29 us (4%)
  between operations  1.57 us (1%)
    ppermute x8, starting transfers between devices, gather_plane(): found[a, 1] = lax.ppermute(line[a], second, down)  19.6 us
    pallas_call x1, Pallas kernels, per_device(): pl.pallas_call(final_kernel, grid=(GQ, 32 // CHUNK), out_shape=sds(GQ, 12...  18.6 us
    ppermute x8, waiting for transfers between devices, gather_plane(): found[a, 3] = lax.ppermute(line[a], second, up)  16.6 us
    pallas_call x1, Pallas kernels, per_device(): pl.pallas_call(measure_kernel, out_shape=[sds(BLOCK_ROWS, 128)] * 8, in_s...  15 us
    ppermute x4, waiting for transfers between devices, gather_plane(): lax.ppermute(found[a, 3], second, up)  12.1 us
    ppermute x7, starting transfers between devices, per_device(): lax.ppermute(blocks[d], ('zh', 'c', 'zl'), [(i, i ^ d) for i in range(8)])  10.4 us
    ppermute x7, waiting for transfers between devices, per_device(): lax.ppermute(blocks[d], ('zh', 'c', 'zl'), [(i, i ^ d) for i in range(8)])  6.88 us
    ppermute x3, waiting for transfers between devices, per_device(): lax.ppermute(lefts[dx], 'x', [(i, (i + dx) % 4) for i in range(4)])  5.58 us
  transfers between devices with their start and end apart: 43, of which 19 were waited for; matrix products, arithmetic and copies ran while one was open for 1% of the time, Pallas kernels for 0%

profile of v1, /device:TPU:0, one launch (start us, length us, event | category | flops | bytes accessed | tf_op | source)
XLA Modules:
  0.0 143.6 jit_solution(2142454908400037720)
XLA Ops:
  1.3 1.3 reshape.6.chosen_ref
  2.6 0.7 select_multiply_fusion
  3.3 0.6 reshape.7.gamma_ref
  4.0 15.0 %measure.1 = (f32[200,128]{1,0:T(8,128)}, f32[200,128]{1,0:T(8,128)}, f32[200,128]{1,0:T(8,128)}, f32[200,128]{1,0:T(8,128)}, f32[200,128]{1,0:T(8,128)}, /*inde...) custom-call(s32[1]{0:T(128)} %bitcast.2.place_ref, s32[1,256]{1,0:T(1,128)} %reshape.6.chosen_ref, ...), custom_call_target="tpu_custom_call" | custom-call | tf_op jit(solution)/shard_map/measure/pallas_call | solution.py:276
  19.0 2.1 %collective-permute-start = (f32[200,128]{1,0:T(8,128)}, f32[200,128]{1,0:T(8,128)S(1)}, u32[]{:S(2)}, u32[]{:S(2)}) collective-permute-start(f32[200,128]{1,0:T(8,128)} %get-tuple-element.20), channel_id=1, source_target_pairs={{0,1},{1,0},{32,33},{33,32},{64,65},{65,64},{96,97},{97,96},{2,3},... | collective-permute-start | bytes 307208 | tf_op jit(solution)/shard_map/ppermute | solution.py:296
  21.1 0.0 collective-permute-start.1
  21.1 0.2 collective-permute-start.2
  21.3 3.9 %collective-permute-start.3 = (f32[200,128]{1,0:T(8,128)}, f32[200,128]{1,0:T(8,128)S(1)}, u32[]{:S(2)}, u32[]{:S(2)}) collective-permute-start(f32[200,128]{1,0:T(8,128)} %get-tuple-element.23), channel_id=1, source_target_pairs={{0,64},{1,65},{32,96},{33,97},{64,0},{65,1},{96,32},{97,33},{2,66}... | collective-permute-start | bytes 307208 | tf_op jit(solution)/shard_map/ppermute | solution.py:296
  25.2 0.7 collective-permute-start.4
  25.9 1.4 collective-permute-start.5
  27.3 2.1 %collective-permute-start.6 = (f32[200,128]{1,0:T(8,128)}, f32[200,128]{1,0:T(8,128)S(1)}, u32[]{:S(2)}, u32[]{:S(2)}) collective-permute-start(f32[200,128]{1,0:T(8,128)} %get-tuple-element.26), channel_id=1, source_target_pairs={{0,97},{1,96},{32,65},{33,64},{64,33},{65,32},{96,1},{97,0},{2,99}... | collective-permute-start | bytes 307208 | tf_op jit(solution)/shard_map/ppermute | solution.py:296
  29.4 0.6 pad_add_fusion.place_ref
  30.0 3.1 %collective-permute-done.3.refs_4_ = f32[200,128]{1,0:T(8,128)S(1)} collective-permute-done((f32[200,128]{1,0:T(8,128)}, f32[200,128]{1,0:T(8,128)S(1)}, u32[]{:S(2)}, u32[]{:S(2)}) %collective-permute-start.3) | collective-permute-done | bytes 102432 | tf_op jit(solution)/shard_map/ppermute | solution.py:296
  33.1 2.9 %collective-permute-done.4.refs_5_ = f32[200,128]{1,0:T(8,128)S(1)} collective-permute-done((f32[200,128]{1,0:T(8,128)}, f32[200,128]{1,0:T(8,128)S(1)}, u32[]{:S(2)}, u32[]{:S(2)}) %collective-permute-start.4) | collective-permute-done | bytes 102432 | tf_op jit(solution)/shard_map/ppermute | solution.py:296
  35.9 0.9 collective-permute-done.6.refs_7_
  36.9 0.6 copy-done.8
  37.5 2.3 %assemble.1 = (f32[520,128]{1,0:T(8,128)}, f32[520,128]{1,0:T(8,128)}, f32[128,128]{1,0:T(8,128)}, f32[128,128]{1,0:T(8,128)}, f32[128,128]{1,0:T(8,128)}, /*index=5*/f32[128,128]{1,0:T(8,128)}) custom-call(s32[2]{0:T(128)} %pad_add_fusion.place_ref, f32[200,128]{1,0:T(8,128)} %get-tuple-element.19.refs_0_, f32[200,128]{1,0:T(8,128)} %copy-done.2, ...), custom_call_target="tpu_custom_call" | custom-call | tf_op jit(solution)/shard_map/assemble/pallas_call | solution.py:299
  39.8 2.8 %collective-permute-start.7 = (f32[128,128]{1,0:T(8,128)}, f32[128,128]{1,0:T(8,128)S(1)}, u32[]{:S(2)}, u32[]{:S(2)}) collective-permute-start(f32[128,128]{1,0:T(8,128)} %get-tuple-element.28), channel_id=1, source_target_pairs={{0,24},{8,0},{16,8},{24,16},{1,25},{9,1},{17,9},{25,17},{2,26},{10... | collective-permute-start | bytes 196616 | tf_op jit(solution)/shard_map/ppermute | solution.py:309
  42.6 0.8 fusion
  43.3 0.8 collective-permute-start.8
  44.2 0.9 collective-permute-start.9
  45.1 4.9 %collective-permute-done.8 = f32[128,128]{1,0:T(8,128)S(1)} collective-permute-done((f32[128,128]{1,0:T(8,128)}, f32[128,128]{1,0:T(8,128)S(1)}, u32[]{:S(2)}, u32[]{:S(2)}) %collective-permute-start.8) | collective-permute-done | bytes 65568 | tf_op jit(solution)/shard_map/ppermute | solution.py:309
  50.0 0.7 collective-permute-done.9
  50.7 3.1 %collective-permute-start.10 = (f32[128,128]{1,0:T(8,128)S(1)}, f32[128,128]{1,0:T(8,128)S(1)}, u32[]{:S(2)}, u32[]{:S(2)}) collective-permute-start(f32[128,128]{1,0:T(8,128)S(1)} %pad_maximum_fusion.1), channel_id=1, source_target_pairs={{0,6},{2,0},{4,2},{6,4},{1,7},{3,1},{5,3},{7,5},{8,14},{10,8},{12,... | collective-permute-start | bytes 196616 | tf_op jit(solution)/shard_map/ppermute | solution.py:313
  53.8 0.6 collective-permute-start.11
  54.4 1.0 collective-permute-start.12
  55.4 1.9 %collective-permute-start.27 = (f32[520,128]{1,0:T(8,128)}, f32[520,128]{1,0:T(8,128)S(1)}, u32[]{:S(2)}, u32[]{:S(2)}) collective-permute-start(f32[520,128]{1,0:T(8,128)} %get-tuple-element.31.refs_4_), channel_id=1, source_target_pairs={{0,2},{2,4},{4,6},{6,0},{1,3},{3,5},{5,7},{7,1},{8,10},{10,12},{12... | collective-permute-start | bytes 798728 | tf_op jit(solution)/shard_map/ppermute | solution.py:264
  57.3 1.3 collective-permute-start.19
  58.6 1.6 %collective-permute-done.11.refs_2_ = f32[128,128]{1,0:T(8,128)S(1)} collective-permute-done((f32[128,128]{1,0:T(8,128)S(1)}, f32[128,128]{1,0:T(8,128)S(1)}, u32[]{:S(2)}, u32[]{:S(2)}) %collective-permute-start.11) | collective-permute-done | bytes 65568 | tf_op jit(solution)/shard_map/ppermute | solution.py:313
  60.2 1.6 %collective-permute-start.13 = (f32[520,128]{1,0:T(8,128)}, f32[520,128]{1,0:T(8,128)S(1)}, u32[]{:S(2)}, u32[]{:S(2)}) collective-permute-start(f32[520,128]{1,0:T(8,128)} %get-tuple-element.31.refs_4_), channel_id=1, source_target_pairs={{0,24},{8,0},{16,8},{24,16},{1,25},{9,1},{17,9},{25,17},{2,26},{10... | collective-permute-start | bytes 798728 | tf_op jit(solution)/shard_map/ppermute | solution.py:259
  61.9 0.7 collective-permute-start.29
  62.5 4.3 %collective-permute-done.27.refs_28_ = f32[520,128]{1,0:T(8,128)S(1)} collective-permute-done((f32[520,128]{1,0:T(8,128)}, f32[520,128]{1,0:T(8,128)S(1)}, u32[]{:S(2)}, u32[]{:S(2)}) %collective-permute-start.27) | collective-permute-done | bytes 266272 | tf_op jit(solution)/shard_map/ppermute | solution.py:264
  66.8 1.1 collective-permute-start.20
  67.9 3.2 %collective-permute-start.14 = (f32[520,128]{1,0:T(8,128)}, f32[520,128]{1,0:T(8,128)S(1)}, u32[]{:S(2)}, u32[]{:S(2)}) collective-permute-start(f32[520,128]{1,0:T(8,128)} %get-tuple-element.32.refs_5_), channel_id=1, source_target_pairs={{0,24},{8,0},{16,8},{24,16},{1,25},{9,1},{17,9},{25,17},{2,26},{10... | collective-permute-start | bytes 798728 | tf_op jit(solution)/shard_map/ppermute | solution.py:265
  71.2 0.9 collective-permute-start.28
  72.1 0.1 collective-permute-start.41
  72.2 1.4 collective-permute-done.20.refs_13_
  73.6 2.2 %collective-permute-start.25 = (f32[520,128]{1,0:T(8,128)S(1)}, f32[520,128]{1,0:T(8,128)S(1)}, u32[]{:S(2)}, u32[]{:S(2)}) collective-permute-start(f32[520,128]{1,0:T(8,128)S(1)} %collective-permute-done.15.refs_10_), channel_id=1, source_target_pairs={{0,6},{2,0},{4,2},{6,4},{1,7},{3,1},{5,3},{7,5},{8,14},{10,8},{12,... | collective-permute-start | bytes 798728 | tf_op jit(solution)/shard_map/ppermute | solution.py:265
  75.8 0.0 collective-permute-done.17.refs_11_
  75.8 0.9 collective-permute-start.38
  76.7 4.9 %collective-permute-done.28.refs_20_ = f32[520,128]{1,0:T(8,128)S(1)} collective-permute-done((f32[520,128]{1,0:T(8,128)S(1)}, f32[520,128]{1,0:T(8,128)S(1)}, u32[]{:S(2)}, u32[]{:S(2)}) %collective-permute-start.28) | collective-permute-done | bytes 266272 | tf_op jit(solution)/shard_map/ppermute | solution.py:266
  81.7 4.8 %collective-permute-done.41.refs_34_ = f32[520,128]{1,0:T(8,128)S(1)} collective-permute-done((f32[520,128]{1,0:T(8,128)S(1)}, f32[520,128]{1,0:T(8,128)S(1)}, u32[]{:S(2)}, u32[]{:S(2)}) %collective-permute-start.41) | collective-permute-done | bytes 266272 | tf_op jit(solution)/shard_map/ppermute | solution.py:264
  86.5 3.2 %collective-permute-start.39 = (f32[520,128]{1,0:T(8,128)S(1)}, f32[520,128]{1,0:T(8,128)S(1)}, u32[]{:S(2)}, u32[]{:S(2)}) collective-permute-start(f32[520,128]{1,0:T(8,128)S(1)} %collective-permute-done.29.refs_29_), channel_id=1, source_target_pairs={{0,24},{8,0},{16,8},{24,16},{1,25},{9,1},{17,9},{25,17},{2,26},{10... | collective-permute-start | bytes 798728 | tf_op jit(solution)/shard_map/ppermute | solution.py:265
  89.7 0.6 collective-permute-start.30
  90.3 1.3 collective-permute-done.38.refs_30_
  91.6 3.2 %collective-permute-start.22 = (f32[520,128]{1,0:T(8,128)S(1)}, f32[520,128]{1,0:T(8,128)S(1)}, u32[]{:S(2)}, u32[]{:S(2)}) collective-permute-start(f32[520,128]{1,0:T(8,128)S(1)} %collective-permute-done.20.refs_13_), channel_id=1, source_target_pairs={{0,24},{8,0},{16,8},{24,16},{1,25},{9,1},{17,9},{25,17},{2,26},{10... | collective-permute-start | bytes 798728 | tf_op jit(solution)/shard_map/ppermute | solution.py:265
  94.9 2.1 %collective-permute-done.42.refs_35_ = f32[520,128]{1,0:T(8,128)S(1)} collective-permute-done((f32[520,128]{1,0:T(8,128)S(1)}, f32[520,128]{1,0:T(8,128)S(1)}, u32[]{:S(2)}, u32[]{:S(2)}) %collective-permute-start.42) | collective-permute-done | bytes 266272 | tf_op jit(solution)/shard_map/ppermute | solution.py:264
  96.9 0.3 collective-permute-start.37
  97.2 2.4 %collective-permute-done.30.refs_21_ = f32[520,128]{1,0:T(8,128)S(1)} collective-permute-done((f32[520,128]{1,0:T(8,128)S(1)}, f32[520,128]{1,0:T(8,128)S(1)}, u32[]{:S(2)}, u32[]{:S(2)}) %collective-permute-start.30) | collective-permute-done | bytes 266272 | tf_op jit(solution)/shard_map/ppermute | solution.py:260
  99.7 0.1 collective-permute-done.26.refs_19_
  99.8 3.1 %collective-permute-start.23 = (f32[520,128]{1,0:T(8,128)S(1)}, f32[520,128]{1,0:T(8,128)S(1)}, u32[]{:S(2)}, u32[]{:S(2)}) collective-permute-start(f32[520,128]{1,0:T(8,128)S(1)} %collective-permute-done.16.refs_8_), channel_id=1, source_target_pairs={{0,6},{2,0},{4,2},{6,4},{1,7},{3,1},{5,3},{7,5},{8,14},{10,8},{12,... | collective-permute-start | bytes 798728 | tf_op jit(solution)/shard_map/ppermute | solution.py:265
  102.9 0.1 collective-permute-start.31
  103.0 3.6 %collective-permute-done.18.refs_9_ = f32[520,128]{1,0:T(8,128)S(1)} collective-permute-done((f32[520,128]{1,0:T(8,128)S(1)}, f32[520,128]{1,0:T(8,128)S(1)}, u32[]{:S(2)}, u32[]{:S(2)}) %collective-permute-start.18) | collective-permute-done | bytes 266272 | tf_op jit(solution)/shard_map/ppermute | solution.py:266
  106.6 3.2 %collective-permute-start.32 = (f32[520,128]{1,0:T(8,128)S(1)}, f32[520,128]{1,0:T(8,128)S(1)}, u32[]{:S(2)}, u32[]{:S(2)}) collective-permute-start(f32[520,128]{1,0:T(8,128)S(1)} %collective-permute-done.30.refs_21_), channel_id=1, source_target_pairs={{0,24},{8,0},{16,8},{24,16},{1,25},{9,1},{17,9},{25,17},{2,26},{10... | collective-permute-start | bytes 798728 | tf_op jit(solution)/shard_map/ppermute | solution.py:265
  109.8 1.1 collective-permute-start.40
  110.9 0.0 collective-permute-start.24
  110.9 0.4 collective-permute-start.34
  111.4 4.0 %collective-permute-done.35.refs_27_ = f32[520,128]{1,0:T(8,128)S(1)} collective-permute-done((f32[520,128]{1,0:T(8,128)S(1)}, f32[520,128]{1,0:T(8,128)S(1)}, u32[]{:S(2)}, u32[]{:S(2)}) %collective-permute-start.35) | collective-permute-done | bytes 266272 | tf_op jit(solution)/shard_map/ppermute | solution.py:264
  115.4 1.2 collective-permute-done.40.refs_33_
  116.6 2.8 %collective-permute-done.24.refs_17_ = f32[520,128]{1,0:T(8,128)S(1)} collective-permute-done((f32[520,128]{1,0:T(8,128)S(1)}, f32[520,128]{1,0:T(8,128)S(1)}, u32[]{:S(2)}, u32[]{:S(2)}) %collective-permute-start.24) | collective-permute-done | bytes 266272 | tf_op jit(solution)/shard_map/ppermute | solution.py:266
  119.5 3.5 %collective-permute-done.36.refs_25_ = f32[520,128]{1,0:T(8,128)S(1)} collective-permute-done((f32[520,128]{1,0:T(8,128)S(1)}, f32[520,128]{1,0:T(8,128)S(1)}, u32[]{:S(2)}, u32[]{:S(2)}) %collective-permute-start.36) | collective-permute-done | bytes 266272 | tf_op jit(solution)/shard_map/ppermute | solution.py:266
  123.0 0.9 copy-done
  124.0 0.9 copy-done.1
  124.9 18.6 %accumulate.1 = f32[4,128,4096]{2,1,0:T(8,128)} custom-call(f32[128,128]{1,0:T(8,128)S(1)} %pad_maximum_fusion.refs_0_, f32[128,128]{1,0:T(8,128)S(1)} %collective-permute-done.10.refs_1_, f32[128,128]{1,0:T(8,128)S(1)} %collective-permute-done.11.refs_2_, f32[128,128]{1,0:T(8,128)S(1)} %collective-permute-done.12.refs_3_, f32[520,128]{1,0:T(8,128)S(1)} %copy-done, ...), custom_call_target="tpu_custom_call" | custom-call | tf_op jit(solution)/shard_map/accumulate/pallas_call | solution.py:319
  (55 shorter events, 0.2 us)
Async XLA Ops:
  19.0 6.9 %collective-permute-start = (f32[200,128]{1,0:T(8,128)}, f32[200,128]{1,0:T(8,128)S(1)}, u32[]{:S(2)}, u32[]{:S(2)}) collective-permute-start(f32[200,128]{1,0:T(8,128)} %get-tuple-element.20), channel_id=1, source_target_pairs={{0,1},{1,0},{32,33},{33,32},{64,65},{65,64},{96,97},{97,96},{2,3},... | collective-permute-start | bytes 307208 | tf_op jit(solution)/shard_map/ppermute | solution.py:296
  21.1 6.2 %collective-permute-start.1 = (f32[200,128]{1,0:T(8,128)}, f32[200,128]{1,0:T(8,128)S(1)}, u32[]{:S(2)}, u32[]{:S(2)}) collective-permute-start(f32[200,128]{1,0:T(8,128)} %get-tuple-element.21), channel_id=1, source_target_pairs={{0,32},{1,33},{32,0},{33,1},{64,96},{65,97},{96,64},{97,65},{2,34}... | collective-permute-start | bytes 307208 | tf_op jit(solution)/shard_map/ppermute | solution.py:296
  21.1 8.9 %collective-permute-start.2 = (f32[200,128]{1,0:T(8,128)}, f32[200,128]{1,0:T(8,128)S(1)}, u32[]{:S(2)}, u32[]{:S(2)}) collective-permute-start(f32[200,128]{1,0:T(8,128)} %get-tuple-element.22), channel_id=1, source_target_pairs={{0,33},{1,32},{32,1},{33,0},{64,97},{65,96},{96,65},{97,64},{2,35}... | collective-permute-start | bytes 307208 | tf_op jit(solution)/shard_map/ppermute | solution.py:296
  21.3 11.8 %collective-permute-start.3 = (f32[200,128]{1,0:T(8,128)}, f32[200,128]{1,0:T(8,128)S(1)}, u32[]{:S(2)}, u32[]{:S(2)}) collective-permute-start(f32[200,128]{1,0:T(8,128)} %get-tuple-element.23), channel_id=1, source_target_pairs={{0,64},{1,65},{32,96},{33,97},{64,0},{65,1},{96,32},{97,33},{2,66}... | collective-permute-start | bytes 307208 | tf_op jit(solution)/shard_map/ppermute | solution.py:296
  25.2 10.7 %collective-permute-start.4 = (f32[200,128]{1,0:T(8,128)}, f32[200,128]{1,0:T(8,128)S(1)}, u32[]{:S(2)}, u32[]{:S(2)}) collective-permute-start(f32[200,128]{1,0:T(8,128)} %get-tuple-element.24), channel_id=1, source_target_pairs={{0,65},{1,64},{32,97},{33,96},{64,1},{65,0},{96,33},{97,32},{2,67}... | collective-permute-start | bytes 307208 | tf_op jit(solution)/shard_map/ppermute | solution.py:296
  25.9 11.0 %copy-start.2 = (f32[200,128]{1,0:T(8,128)}, f32[200,128]{1,0:T(8,128)S(1)}, u32[]{:S(2)}) copy-start(f32[200,128]{1,0:T(8,128)S(1)} %collective-permute-done.refs_1_) | copy-start | bytes 307204
  25.9 10.0 %collective-permute-start.5 = (f32[200,128]{1,0:T(8,128)}, f32[200,128]{1,0:T(8,128)S(1)}, u32[]{:S(2)}, u32[]{:S(2)}) collective-permute-start(f32[200,128]{1,0:T(8,128)} %get-tuple-element.25), channel_id=1, source_target_pairs={{0,96},{1,97},{32,64},{33,65},{64,32},{65,33},{96,0},{97,1},{2,98}... | collective-permute-start | bytes 307208 | tf_op jit(solution)/shard_map/ppermute | solution.py:296
  27.3 9.6 %copy-start.3 = (f32[200,128]{1,0:T(8,128)}, f32[200,128]{1,0:T(8,128)S(1)}, u32[]{:S(2)}) copy-start(f32[200,128]{1,0:T(8,128)S(1)} %collective-permute-done.1.refs_2_) | copy-start | bytes 307204
  27.3 9.6 %collective-permute-start.6 = (f32[200,128]{1,0:T(8,128)}, f32[200,128]{1,0:T(8,128)S(1)}, u32[]{:S(2)}, u32[]{:S(2)}) collective-permute-start(f32[200,128]{1,0:T(8,128)} %get-tuple-element.26), channel_id=1, source_target_pairs={{0,97},{1,96},{32,65},{33,64},{64,33},{65,32},{96,1},{97,0},{2,99}... | collective-permute-start | bytes 307208 | tf_op jit(solution)/shard_map/ppermute | solution.py:296
  30.0 6.9 %copy-start.4 = (f32[200,128]{1,0:T(8,128)}, f32[200,128]{1,0:T(8,128)S(1)}, u32[]{:S(2)}) copy-start(f32[200,128]{1,0:T(8,128)S(1)} %collective-permute-done.2.refs_3_) | copy-start | bytes 307204
  33.1 3.8 %copy-start.5 = (f32[200,128]{1,0:T(8,128)}, f32[200,128]{1,0:T(8,128)S(1)}, u32[]{:S(2)}) copy-start(f32[200,128]{1,0:T(8,128)S(1)} %collective-permute-done.3.refs_4_) | copy-start | bytes 307204
  35.9 1.0 copy-start.6
  35.9 1.0 copy-start.7
  36.9 0.6 copy-start.8
  39.8 5.3 %collective-permute-start.7 = (f32[128,128]{1,0:T(8,128)}, f32[128,128]{1,0:T(8,128)S(1)}, u32[]{:S(2)}, u32[]{:S(2)}) collective-permute-start(f32[128,128]{1,0:T(8,128)} %get-tuple-element.28), channel_id=1, source_target_pairs={{0,24},{8,0},{16,8},{24,16},{1,25},{9,1},{17,9},{25,17},{2,26},{10... | collective-permute-start | bytes 196616 | tf_op jit(solution)/shard_map/ppermute | solution.py:309
  43.3 6.6 %collective-permute-start.8 = (f32[128,128]{1,0:T(8,128)}, f32[128,128]{1,0:T(8,128)S(1)}, u32[]{:S(2)}, u32[]{:S(2)}) collective-permute-start(f32[128,128]{1,0:T(8,128)} %get-tuple-element.29), channel_id=1, source_target_pairs={{0,16},{8,24},{16,0},{24,8},{1,17},{9,25},{17,1},{25,9},{2,18},{10... | collective-permute-start | bytes 196616 | tf_op jit(solution)/shard_map/ppermute | solution.py:309
  44.2 6.5 %collective-permute-start.9 = (f32[128,128]{1,0:T(8,128)}, f32[128,128]{1,0:T(8,128)S(1)}, u32[]{:S(2)}, u32[]{:S(2)}) collective-permute-start(f32[128,128]{1,0:T(8,128)} %get-tuple-element.30), channel_id=1, source_target_pairs={{0,8},{8,16},{16,24},{24,0},{1,9},{9,17},{17,25},{25,1},{2,10},{10... | collective-permute-start | bytes 196616 | tf_op jit(solution)/shard_map/ppermute | solution.py:309
  50.7 7.9 %collective-permute-start.10 = (f32[128,128]{1,0:T(8,128)S(1)}, f32[128,128]{1,0:T(8,128)S(1)}, u32[]{:S(2)}, u32[]{:S(2)}) collective-permute-start(f32[128,128]{1,0:T(8,128)S(1)} %pad_maximum_fusion.1), channel_id=1, source_target_pairs={{0,6},{2,0},{4,2},{6,4},{1,7},{3,1},{5,3},{7,5},{8,14},{10,8},{12,... | collective-permute-start | bytes 196616 | tf_op jit(solution)/shard_map/ppermute | solution.py:313
  53.8 6.5 %collective-permute-start.11 = (f32[128,128]{1,0:T(8,128)S(1)}, f32[128,128]{1,0:T(8,128)S(1)}, u32[]{:S(2)}, u32[]{:S(2)}) collective-permute-start(f32[128,128]{1,0:T(8,128)S(1)} %pad_maximum_fusion.2), channel_id=1, source_target_pairs={{0,4},{2,6},{4,0},{6,2},{1,5},{3,7},{5,1},{7,3},{8,12},{10,14},{12... | collective-permute-start | bytes 196616 | tf_op jit(solution)/shard_map/ppermute | solution.py:313
  54.4 7.5 %collective-permute-start.12 = (f32[128,128]{1,0:T(8,128)S(1)}, f32[128,128]{1,0:T(8,128)S(1)}, u32[]{:S(2)}, u32[]{:S(2)}) collective-permute-start(f32[128,128]{1,0:T(8,128)S(1)} %pad_maximum_fusion.3), channel_id=1, source_target_pairs={{0,2},{2,4},{4,6},{6,0},{1,3},{3,5},{5,7},{7,1},{8,10},{10,12},{12... | collective-permute-start | bytes 196616 | tf_op jit(solution)/shard_map/ppermute | solution.py:313
  55.4 11.4 %collective-permute-start.27 = (f32[520,128]{1,0:T(8,128)}, f32[520,128]{1,0:T(8,128)S(1)}, u32[]{:S(2)}, u32[]{:S(2)}) collective-permute-start(f32[520,128]{1,0:T(8,128)} %get-tuple-element.31.refs_4_), channel_id=1, source_target_pairs={{0,2},{2,4},{4,6},{6,0},{1,3},{3,5},{5,7},{7,1},{8,10},{10,12},{12... | collective-permute-start | bytes 798728 | tf_op jit(solution)/shard_map/ppermute | solution.py:264
  57.3 10.7 %collective-permute-start.19 = (f32[520,128]{1,0:T(8,128)}, f32[520,128]{1,0:T(8,128)S(1)}, u32[]{:S(2)}, u32[]{:S(2)}) collective-permute-start(f32[520,128]{1,0:T(8,128)} %get-tuple-element.31.refs_4_), channel_id=1, source_target_pairs={{0,6},{2,0},{4,2},{6,4},{1,7},{3,1},{5,3},{7,5},{8,14},{10,8},{12,... | collective-permute-start | bytes 798728 | tf_op jit(solution)/shard_map/ppermute | solution.py:265
  58.6 9.3 %collective-permute-start.15 = (f32[520,128]{1,0:T(8,128)}, f32[520,128]{1,0:T(8,128)S(1)}, u32[]{:S(2)}, u32[]{:S(2)}) collective-permute-start(f32[520,128]{1,0:T(8,128)} %get-tuple-element.31.refs_4_), channel_id=1, source_target_pairs={{0,8},{8,16},{16,24},{24,0},{1,9},{9,17},{17,25},{25,1},{2,10},{10... | collective-permute-start | bytes 798728 | tf_op jit(solution)/shard_map/ppermute | solution.py:259
  60.2 10.9 %collective-permute-start.13 = (f32[520,128]{1,0:T(8,128)}, f32[520,128]{1,0:T(8,128)S(1)}, u32[]{:S(2)}, u32[]{:S(2)}) collective-permute-start(f32[520,128]{1,0:T(8,128)} %get-tuple-element.31.refs_4_), channel_id=1, source_target_pairs={{0,24},{8,0},{16,8},{24,16},{1,25},{9,1},{17,9},{25,17},{2,26},{10... | collective-permute-start | bytes 798728 | tf_op jit(solution)/shard_map/ppermute | solution.py:259
  61.9 10.2 %collective-permute-start.29 = (f32[520,128]{1,0:T(8,128)}, f32[520,128]{1,0:T(8,128)S(1)}, u32[]{:S(2)}, u32[]{:S(2)}) collective-permute-start(f32[520,128]{1,0:T(8,128)} %get-tuple-element.32.refs_5_), channel_id=1, source_target_pairs={{0,2},{2,4},{4,6},{6,0},{1,3},{3,5},{5,7},{7,1},{8,10},{10,12},{12... | collective-permute-start | bytes 798728 | tf_op jit(solution)/shard_map/ppermute | solution.py:259
  66.8 6.8 %collective-permute-start.20 = (f32[520,128]{1,0:T(8,128)}, f32[520,128]{1,0:T(8,128)S(1)}, u32[]{:S(2)}, u32[]{:S(2)}) collective-permute-start(f32[520,128]{1,0:T(8,128)} %get-tuple-element.32.refs_5_), channel_id=1, source_target_pairs={{0,6},{2,0},{4,2},{6,4},{1,7},{3,1},{5,3},{7,5},{8,14},{10,8},{12,... | collective-permute-start | bytes 798728 | tf_op jit(solution)/shard_map/ppermute | solution.py:259
  67.9 7.8 %collective-permute-start.17 = (f32[520,128]{1,0:T(8,128)}, f32[520,128]{1,0:T(8,128)S(1)}, u32[]{:S(2)}, u32[]{:S(2)}) collective-permute-start(f32[520,128]{1,0:T(8,128)} %get-tuple-element.32.refs_5_), channel_id=1, source_target_pairs={{0,8},{8,16},{16,24},{24,0},{1,9},{9,17},{17,25},{25,1},{2,10},{10... | collective-permute-start | bytes 798728 | tf_op jit(solution)/shard_map/ppermute | solution.py:264
  67.9 7.8 %collective-permute-start.14 = (f32[520,128]{1,0:T(8,128)}, f32[520,128]{1,0:T(8,128)S(1)}, u32[]{:S(2)}, u32[]{:S(2)}) collective-permute-start(f32[520,128]{1,0:T(8,128)} %get-tuple-element.32.refs_5_), channel_id=1, source_target_pairs={{0,24},{8,0},{16,8},{24,16},{1,25},{9,1},{17,9},{25,17},{2,26},{10... | collective-permute-start | bytes 798728 | tf_op jit(solution)/shard_map/ppermute | solution.py:265
  71.2 10.5 %collective-permute-start.28 = (f32[520,128]{1,0:T(8,128)S(1)}, f32[520,128]{1,0:T(8,128)S(1)}, u32[]{:S(2)}, u32[]{:S(2)}) collective-permute-start(f32[520,128]{1,0:T(8,128)S(1)} %collective-permute-done.27.refs_28_), channel_id=1, source_target_pairs={{0,2},{2,4},{4,6},{6,0},{1,3},{3,5},{5,7},{7,1},{8,10},{10,12},{12... | collective-permute-start | bytes 798728 | tf_op jit(solution)/shard_map/ppermute | solution.py:266
  72.1 14.4 %collective-permute-start.41 = (f32[520,128]{1,0:T(8,128)S(1)}, f32[520,128]{1,0:T(8,128)S(1)}, u32[]{:S(2)}, u32[]{:S(2)}) collective-permute-start(f32[520,128]{1,0:T(8,128)S(1)} %collective-permute-done.15.refs_10_), channel_id=1, source_target_pairs={{0,2},{2,4},{4,6},{6,0},{1,3},{3,5},{5,7},{7,1},{8,10},{10,12},{12... | collective-permute-start | bytes 798728 | tf_op jit(solution)/shard_map/ppermute | solution.py:264
  73.6 12.9 %collective-permute-start.25 = (f32[520,128]{1,0:T(8,128)S(1)}, f32[520,128]{1,0:T(8,128)S(1)}, u32[]{:S(2)}, u32[]{:S(2)}) collective-permute-start(f32[520,128]{1,0:T(8,128)S(1)} %collective-permute-done.15.refs_10_), channel_id=1, source_target_pairs={{0,6},{2,0},{4,2},{6,4},{1,7},{3,1},{5,3},{7,5},{8,14},{10,8},{12,... | collective-permute-start | bytes 798728 | tf_op jit(solution)/shard_map/ppermute | solution.py:265
  75.8 13.9 %collective-permute-start.16 = (f32[520,128]{1,0:T(8,128)S(1)}, f32[520,128]{1,0:T(8,128)S(1)}, u32[]{:S(2)}, u32[]{:S(2)}) collective-permute-start(f32[520,128]{1,0:T(8,128)S(1)} %collective-permute-done.15.refs_10_), channel_id=1, source_target_pairs={{0,8},{8,16},{16,24},{24,0},{1,9},{9,17},{17,25},{25,1},{2,10},{10... | collective-permute-start | bytes 798728 | tf_op jit(solution)/shard_map/ppermute | solution.py:260
  75.8 15.8 %collective-permute-start.38 = (f32[520,128]{1,0:T(8,128)S(1)}, f32[520,128]{1,0:T(8,128)S(1)}, u32[]{:S(2)}, u32[]{:S(2)}) collective-permute-start(f32[520,128]{1,0:T(8,128)S(1)} %collective-permute-done.13.refs_6_), channel_id=1, source_target_pairs={{0,2},{2,4},{4,6},{6,0},{1,3},{3,5},{5,7},{7,1},{8,10},{10,12},{12... | collective-permute-start | bytes 798728 | tf_op jit(solution)/shard_map/ppermute | solution.py:264
  81.6 10.0 %collective-permute-start.21 = (f32[520,128]{1,0:T(8,128)S(1)}, f32[520,128]{1,0:T(8,128)S(1)}, u32[]{:S(2)}, u32[]{:S(2)}) collective-permute-start(f32[520,128]{1,0:T(8,128)S(1)} %collective-permute-done.13.refs_6_), channel_id=1, source_target_pairs={{0,6},{2,0},{4,2},{6,4},{1,7},{3,1},{5,3},{7,5},{8,14},{10,8},{12,... | collective-permute-start | bytes 798728 | tf_op jit(solution)/shard_map/ppermute | solution.py:265
  86.5 10.5 %collective-permute-start.42 = (f32[520,128]{1,0:T(8,128)S(1)}, f32[520,128]{1,0:T(8,128)S(1)}, u32[]{:S(2)}, u32[]{:S(2)}) collective-permute-start(f32[520,128]{1,0:T(8,128)S(1)} %collective-permute-done.29.refs_29_), channel_id=1, source_target_pairs={{0,8},{8,16},{16,24},{24,0},{1,9},{9,17},{17,25},{25,1},{2,10},{10... | collective-permute-start | bytes 798728 | tf_op jit(solution)/shard_map/ppermute | solution.py:264
  86.5 10.5 %collective-permute-start.39 = (f32[520,128]{1,0:T(8,128)S(1)}, f32[520,128]{1,0:T(8,128)S(1)}, u32[]{:S(2)}, u32[]{:S(2)}) collective-permute-start(f32[520,128]{1,0:T(8,128)S(1)} %collective-permute-done.29.refs_29_), channel_id=1, source_target_pairs={{0,24},{8,0},{16,8},{24,16},{1,25},{9,1},{17,9},{25,17},{2,26},{10... | collective-permute-start | bytes 798728 | tf_op jit(solution)/shard_map/ppermute | solution.py:265
  89.7 10.0 %collective-permute-start.30 = (f32[520,128]{1,0:T(8,128)S(1)}, f32[520,128]{1,0:T(8,128)S(1)}, u32[]{:S(2)}, u32[]{:S(2)}) collective-permute-start(f32[520,128]{1,0:T(8,128)S(1)} %collective-permute-done.29.refs_29_), channel_id=1, source_target_pairs={{0,2},{2,4},{4,6},{6,0},{1,3},{3,5},{5,7},{7,1},{8,10},{10,12},{12... | collective-permute-start | bytes 798728 | tf_op jit(solution)/shard_map/ppermute | solution.py:260
  91.6 8.2 %collective-permute-start.26 = (f32[520,128]{1,0:T(8,128)S(1)}, f32[520,128]{1,0:T(8,128)S(1)}, u32[]{:S(2)}, u32[]{:S(2)}) collective-permute-start(f32[520,128]{1,0:T(8,128)S(1)} %collective-permute-done.20.refs_13_), channel_id=1, source_target_pairs={{0,8},{8,16},{16,24},{24,0},{1,9},{9,17},{17,25},{25,1},{2,10},{10... | collective-permute-start | bytes 798728 | tf_op jit(solution)/shard_map/ppermute | solution.py:264
  91.6 11.3 %collective-permute-start.22 = (f32[520,128]{1,0:T(8,128)S(1)}, f32[520,128]{1,0:T(8,128)S(1)}, u32[]{:S(2)}, u32[]{:S(2)}) collective-permute-start(f32[520,128]{1,0:T(8,128)S(1)} %collective-permute-done.20.refs_13_), channel_id=1, source_target_pairs={{0,24},{8,0},{16,8},{24,16},{1,25},{9,1},{17,9},{25,17},{2,26},{10... | collective-permute-start | bytes 798728 | tf_op jit(solution)/shard_map/ppermute | solution.py:265
  96.9 9.7 %collective-permute-start.18 = (f32[520,128]{1,0:T(8,128)S(1)}, f32[520,128]{1,0:T(8,128)S(1)}, u32[]{:S(2)}, u32[]{:S(2)}) collective-permute-start(f32[520,128]{1,0:T(8,128)S(1)} %collective-permute-done.17.refs_11_), channel_id=1, source_target_pairs={{0,8},{8,16},{16,24},{24,0},{1,9},{9,17},{17,25},{25,1},{2,10},{10... | collective-permute-start | bytes 798728 | tf_op jit(solution)/shard_map/ppermute | solution.py:266
  96.9 9.7 %collective-permute-start.37 = (f32[520,128]{1,0:T(8,128)S(1)}, f32[520,128]{1,0:T(8,128)S(1)}, u32[]{:S(2)}, u32[]{:S(2)}) collective-permute-start(f32[520,128]{1,0:T(8,128)S(1)} %collective-permute-done.25.refs_18_), channel_id=1, source_target_pairs={{0,6},{2,0},{4,2},{6,4},{1,7},{3,1},{5,3},{7,5},{8,14},{10,8},{12,... | collective-permute-start | bytes 798728 | tf_op jit(solution)/shard_map/ppermute | solution.py:266
  99.7 10.2 %collective-permute-start.33 = (f32[520,128]{1,0:T(8,128)S(1)}, f32[520,128]{1,0:T(8,128)S(1)}, u32[]{:S(2)}, u32[]{:S(2)}) collective-permute-start(f32[520,128]{1,0:T(8,128)S(1)} %collective-permute-done.16.refs_8_), channel_id=1, source_target_pairs={{0,2},{2,4},{4,6},{6,0},{1,3},{3,5},{5,7},{7,1},{8,10},{10,12},{12... | collective-permute-start | bytes 798728 | tf_op jit(solution)/shard_map/ppermute | solution.py:264
  99.8 11.1 %collective-permute-start.23 = (f32[520,128]{1,0:T(8,128)S(1)}, f32[520,128]{1,0:T(8,128)S(1)}, u32[]{:S(2)}, u32[]{:S(2)}) collective-permute-start(f32[520,128]{1,0:T(8,128)S(1)} %collective-permute-done.16.refs_8_), channel_id=1, source_target_pairs={{0,6},{2,0},{4,2},{6,4},{1,7},{3,1},{5,3},{7,5},{8,14},{10,8},{12,... | collective-permute-start | bytes 798728 | tf_op jit(solution)/shard_map/ppermute | solution.py:265
  102.9 8.0 %collective-permute-start.31 = (f32[520,128]{1,0:T(8,128)S(1)}, f32[520,128]{1,0:T(8,128)S(1)}, u32[]{:S(2)}, u32[]{:S(2)}) collective-permute-start(f32[520,128]{1,0:T(8,128)S(1)} %collective-permute-done.21.refs_14_), channel_id=1, source_target_pairs={{0,6},{2,0},{4,2},{6,4},{1,7},{3,1},{5,3},{7,5},{8,14},{10,8},{12,... | collective-permute-start | bytes 798728 | tf_op jit(solution)/shard_map/ppermute | solution.py:266
  106.6 8.8 %collective-permute-start.35 = (f32[520,128]{1,0:T(8,128)S(1)}, f32[520,128]{1,0:T(8,128)S(1)}, u32[]{:S(2)}, u32[]{:S(2)}) collective-permute-start(f32[520,128]{1,0:T(8,128)S(1)} %collective-permute-done.30.refs_21_), channel_id=1, source_target_pairs={{0,8},{8,16},{16,24},{24,0},{1,9},{9,17},{17,25},{25,1},{2,10},{10... | collective-permute-start | bytes 798728 | tf_op jit(solution)/shard_map/ppermute | solution.py:264
  106.6 10.0 %collective-permute-start.32 = (f32[520,128]{1,0:T(8,128)S(1)}, f32[520,128]{1,0:T(8,128)S(1)}, u32[]{:S(2)}, u32[]{:S(2)}) collective-permute-start(f32[520,128]{1,0:T(8,128)S(1)} %collective-permute-done.30.refs_21_), channel_id=1, source_target_pairs={{0,24},{8,0},{16,8},{24,16},{1,25},{9,1},{17,9},{25,17},{2,26},{10... | collective-permute-start | bytes 798728 | tf_op jit(solution)/shard_map/ppermute | solution.py:265
  109.8 6.8 %collective-permute-start.40 = (f32[520,128]{1,0:T(8,128)S(1)}, f32[520,128]{1,0:T(8,128)S(1)}, u32[]{:S(2)}, u32[]{:S(2)}) collective-permute-start(f32[520,128]{1,0:T(8,128)S(1)} %collective-permute-done.39.refs_31_), channel_id=1, source_target_pairs={{0,24},{8,0},{16,8},{24,16},{1,25},{9,1},{17,9},{25,17},{2,26},{10... | collective-permute-start | bytes 798728 | tf_op jit(solution)/shard_map/ppermute | solution.py:266
  110.9 8.5 %collective-permute-start.24 = (f32[520,128]{1,0:T(8,128)S(1)}, f32[520,128]{1,0:T(8,128)S(1)}, u32[]{:S(2)}, u32[]{:S(2)}) collective-permute-start(f32[520,128]{1,0:T(8,128)S(1)} %collective-permute-done.22.refs_15_), channel_id=1, source_target_pairs={{0,24},{8,0},{16,8},{24,16},{1,25},{9,1},{17,9},{25,17},{2,26},{10... | collective-permute-start | bytes 798728 | tf_op jit(solution)/shard_map/ppermute | solution.py:266
  110.9 8.5 %collective-permute-start.34 = (f32[520,128]{1,0:T(8,128)S(1)}, f32[520,128]{1,0:T(8,128)S(1)}, u32[]{:S(2)}, u32[]{:S(2)}) collective-permute-start(f32[520,128]{1,0:T(8,128)S(1)} %collective-permute-done.33.refs_32_), channel_id=1, source_target_pairs={{0,2},{2,4},{4,6},{6,0},{1,3},{3,5},{5,7},{7,1},{8,10},{10,12},{12... | collective-permute-start | bytes 798728 | tf_op jit(solution)/shard_map/ppermute | solution.py:266
  115.4 7.6 %collective-permute-start.36 = (f32[520,128]{1,0:T(8,128)S(1)}, f32[520,128]{1,0:T(8,128)S(1)}, u32[]{:S(2)}, u32[]{:S(2)}) collective-permute-start(f32[520,128]{1,0:T(8,128)S(1)} %collective-permute-done.35.refs_27_), channel_id=1, source_target_pairs={{0,8},{8,16},{16,24},{24,0},{1,9},{9,17},{17,25},{25,1},{2,10},{10... | collective-permute-start | bytes 798728 | tf_op jit(solution)/shard_map/ppermute | solution.py:266
  123.0 1.0 copy-start
  124.0 1.0 copy-start.1

commit v2 on v1

v2 whole, which is shorter than its diff:
```python
import jax
import jax.numpy as jnp
import numpy as np
from jax import lax
from jax.experimental import pallas as pl
from jax.experimental.pallas import tpu as pltpu
from jax.sharding import Mesh
from jax.sharding import PartitionSpec as P


K = 1024
SITES = 64
LEG = 64
Q = 16
TIMES = 4096
UPDATES = 4
RANKB = 64
NS = UPDATES * RANKB
GQ = 4
RIGHT_ROWS = GQ * 32
LEFT_ROWS = GQ * 16
BLOCK_ROWS = RIGHT_ROWS + LEFT_ROWS + 8
F32 = jnp.float32
BF16 = jnp.bfloat16
NN = (((1,), (0,)), ((), ()))
NT = (((1,), (1,)), ((), ()))
TN = (((0,), (0,)), ((), ()))
MIB = 1 << 20


def mm(a, b, dims=NN):
    return lax.dot_general(a, b, dims, preferred_element_type=F32)


def split2(x):
    hi = x.astype(BF16)
    return hi, (x - hi.astype(F32)).astype(BF16)


def split3(x):
    hi = x.astype(BF16)
    rest = x - hi.astype(F32)
    mid = rest.astype(BF16)
    return hi, mid, (rest - mid.astype(F32)).astype(BF16)


def mm3(a, b, dims=NN):
    ah, al = a if isinstance(a, tuple) else split2(a)
    bh, bl = b if isinstance(b, tuple) else split2(b)
    rows = ah.shape[0]
    top = mm(jnp.concatenate([ah, al], axis=0), bh, dims)
    return top[:rows] + (top[rows:] + mm(ah, bl, dims))


def iota(shape, dim):
    return lax.broadcasted_iota(jnp.int32, shape, dim)


def row_to_column(row):
    n = row.shape[1]
    same = iota((n, n), 0) == iota((n, n), 1)
    return jnp.sum(jnp.where(same, row, jnp.zeros_like(row)), axis=1, keepdims=True)


def measure_kernel(
    chosen_ref, spin_ref, accept_ref, site_ref, time_ref, left_ref, right_ref, weight_ref, routing_ref, perturb_ref,
    *rest,
):
    outs = rest[:8]
    (matrix, p_hi, p_lo, polys, spread, vecs, left_meas, right_meas, sem) = rest[8:]
    load = pltpu.make_async_copy(perturb_ref.at[0], matrix, sem)
    load.start()

    abscissa = (2.0 * time_ref[...].astype(F32) + 1.0) / TIMES - 1.0
    before, now = jnp.ones_like(abscissa), abscissa
    polys[0:1, :] = before
    polys[1:2, :] = now * float(np.sqrt(3.0))
    for degree in range(1, LEG - 1):
        after = abscissa * now * ((2 * degree + 1) / (degree + 1)) - before * (degree / (degree + 1))
        before, now = now, after
        polys[degree + 1 : degree + 2, :] = now * float(np.sqrt(2.0 * degree + 3.0))

    sites = site_ref[...]
    onehot = (iota((SITES, K), 0) == sites).astype(F32).astype(BF16)
    onehot3 = jnp.concatenate([onehot, onehot, onehot], axis=0)
    for side, table_ref in ((0, left_ref), (1, right_ref)):
        table = jnp.concatenate(split3(table_ref[...]), axis=0)
        spread[...] = mm(table, onehot3, TN)
        total = jnp.zeros((Q, K), F32)
        for degree in range(LEG):
            total = total + spread[degree * Q : (degree + 1) * Q, :] * polys[degree : degree + 1, :]
        vecs[side] = total

    def one_row(values):
        return jnp.concatenate([values[u : u + 1, :] for u in range(UPDATES)], axis=1)

    chosen = row_to_column(one_row(chosen_ref[0].astype(F32))).astype(jnp.int32)
    pick = (iota((NS, K), 1) == chosen).astype(F32).astype(BF16)
    gamma = one_row(accept_ref[0].astype(F32) * jnp.where(spin_ref[0] == 1, 0.6, -0.4))
    gamma_column = row_to_column(gamma)
    load.wait()
    for step in range(4):
        rows = slice(step * 256, (step + 1) * 256)
        hi, lo = split2(matrix[rows, :])
        p_hi[rows, :] = hi
        p_lo[rows, :] = lo
    ph, plo = p_hi[...], p_lo[...]
    v, w = vecs[0], vecs[1]
    wh, wl = split2(w)
    high = mm(jnp.concatenate([pick, wh, wl], axis=0), ph)
    low = mm(jnp.concatenate([pick, wh], axis=0), plo)
    rows_hi, rows_lo = high[:NS].astype(BF16), low[:NS].astype(BF16)
    from_w = high[NS : NS + Q] + high[NS + Q :] + low[NS:]
    same = mm(pick, pick, NT)
    small = mm(rows_hi, pick, NT) + mm(rows_lo, pick, NT)
    vs = split3(v)
    p_vec = mm(pick, vs[0], NT) + mm(pick, vs[1], NT) + mm(pick, vs[2], NT)
    p_vec = p_vec + mm3((rows_hi, rows_lo), (vs[0], vs[1]), NT)
    fs = split3(from_w)
    q_vec = mm(fs[0], pick, NT) + mm(fs[1], pick, NT) + mm(fs[2], pick, NT)
    row_block = lax.div(iota((NS, NS), 0), RANKB)
    col_block = lax.div(iota((NS, NS), 1), RANKB)
    c_all, r_all = jnp.zeros((NS, NS), F32), jnp.zeros((NS, NS), F32)
    x, y = jnp.zeros((NS, Q), F32), jnp.zeros((Q, NS), F32)
    for update in range(UPDATES):
        mine = col_block == update
        columns = jnp.where(mine, small * gamma, 0.0)
        y_now = jnp.where(mine[:Q], q_vec * gamma, 0.0)
        rows_now = small + same
        x = jnp.where(row_block[:, :Q] == update, p_vec, x)
        y = y + y_now
        if update < UPDATES - 1:
            c_all = c_all + columns
            r_all = jnp.where(row_block == update, rows_now, r_all)
            change = mm3(jnp.concatenate([columns, y_now], axis=0), rows_now)
            p_vec = p_vec - mm3(columns, p_vec)
            small = small - change[:NS]
            q_vec = q_vec - change[NS:]
    lower = split2(jnp.where(row_block > col_block, c_all, 0.0))
    upper = split2(jnp.where(row_block < col_block, r_all, 0.0) * gamma)
    lower_twice, upper_twice = split2(mm3(lower, lower)), split2(mm3(upper, upper))
    z = x + mm3(upper_twice, x)
    y2 = y + mm3(y, lower_twice)
    z = z - mm3(upper, z)
    y2 = y2 - mm3(y2, lower)
    zs, ys = split3(z * gamma_column), split3(y2)
    left_arg = v - (mm(zs[0], pick, TN) + mm(zs[1], pick, TN) + mm(zs[2], pick, TN))
    left_image = v + mm3(left_arg, (ph, plo), NT)
    right_arg = w - (mm(ys[0], pick) + mm(ys[1], pick) + mm(ys[2], pick))
    right_image = right_arg + from_w - mm3((ys[0], ys[1]), (rows_hi, rows_lo))

    odd = lax.rem(sites, 2).astype(F32)
    values = polys[...]
    values = jnp.concatenate([values * (1.0 - odd), values * odd], axis=0)
    both = jnp.concatenate(split2(values), axis=0)
    pair = iota((32, K), 0) == lax.div(sites, 2)
    for image, meas in ((right_image, right_meas), (left_image, left_meas)):
        ih = image.astype(BF16).astype(F32)
        il = image - ih

        def masked(part):
            return jnp.concatenate(
                [jnp.where(pair, part[q : q + 1, :], 0.0).astype(BF16) for q in range(Q)], axis=0
            )

        high = mm(masked(ih), both, NT)
        low = mm(masked(il), both[:128], NT)
        meas[...] = high[:, :128] + (high[:, 128:] + low)

    lane = iota((8, 128), 1)
    own_group = lax.axis_index("zh") * 2 + lax.axis_index("c")
    key = (routing_ref[0, 0] + 32 * own_group).astype(F32)
    meta = jnp.where(lane == 0, weight_ref[0], jnp.where(lane == 1, key, 0.0))
    for distance in range(8):
        target = (own_group * 2 + lax.axis_index("zl")) ^ distance
        group, half = target // 2, target % 2
        first = pl.multiple_of(group * RIGHT_ROWS, RIGHT_ROWS)
        outs[distance][0:RIGHT_ROWS, :] = right_meas[pl.ds(first, RIGHT_ROWS), :]
        outs[distance][RIGHT_ROWS : RIGHT_ROWS + LEFT_ROWS, :] = left_meas[pl.ds(first + half, LEFT_ROWS, stride=2), :]
        outs[distance][RIGHT_ROWS + LEFT_ROWS :, :] = meta


TILE_META = 64
HALF = 32


def assemble_kernel(*refs):
    blocks, outs = refs[:8], (refs[8:11], refs[11:14])
    place = (lax.axis_index("x"), lax.axis_index("y"))
    for colour in range(2):
        up, down, own = outs[colour]
        size = 65 - colour
        for d in range(8):
            rows = blocks[d][colour * 64 : (colour + 1) * 64, :]
            up[0:64, d, :] = rows
            down[0:64, d, :] = rows
            if colour == 0:
                first = RIGHT_ROWS + LEFT_ROWS
                up[TILE_META, d : d + 1, :] = blocks[d][first : first + 1, :]
                down[TILE_META, d : d + 1, :] = blocks[d][first : first + 1, :]

        def fill(ref, at, along, across):
            shift = (along, across) if colour == 0 else (across, along)
            owner = ((place[0] + shift[0]) % 4) * 4 + (place[1] + shift[1]) % 4
            for d in range(8):
                rows = blocks[d][pl.ds(RIGHT_ROWS + colour * 32 + owner, 2, stride=16), :]
                ref[at, d : d + 1, :] = rows[0:1]
                ref[at + 1, d : d + 1, :] = rows[1:2]

        for across in range(4):
            fill(up, size + 2 * across, 1, across)
            fill(down, size + 2 * across, 3, across)
            fill(own, 2 * across, 0, across)
        for k in range(2):
            fill(up, size + 8 + 2 * k, 2, k)
            fill(down, size + 8 + 2 * k, 2, 2 + k)


CHUNK = 8
STEPS = 32 // CHUNK


def find_tiles(colour):
    n = 65 - colour
    P, OWN, A, B, C, D, E, F, G, H, I, J = range(12)
    right = {
        (0, 0): ((P, 0), (P, HALF)),
        (3, 0): ((A, 0), (A, HALF)),
        (1, 0): ((B, 0), (B, HALF)),
        (2, 0): ((C, 0), (D, 0)),
        (0, 2): ((I, 0), (I, HALF)),
        (3, 2): ((I, n), (J, 0)),
        (1, 2): ((J, n - HALF), (J, n)),
        (2, 2): ((I, n + HALF), (J, 2 * n - HALF)),
    }
    left = {
        (0, 0): (OWN, 0),
        (3, 0): (A, n),
        (1, 0): (B, n),
        (2, 0): (C, HALF),
        (0, 2): (I, n + 2 * HALF),
        (3, 2): (I, n + 2 * HALF + 2),
        (1, 2): (J, 3 * n - 2 * HALF),
        (2, 2): (J, 3 * n - 2 * HALF + 2),
    }
    for across, near, far in ((3, E, G), (1, F, H)):
        for i, along in enumerate((0, 3, 1)):
            right[along, across] = ((near, i * n), (near, i * n + HALF))
        right[2, across] = ((far, 0), (far, HALF))
        for i, along in enumerate((0, 3, 1, 2)):
            left[along, across] = (far, n + 2 * i)
    order = [(sx, sy) for sy in range(4) for sx in range(4)]
    if colour == 1:
        order = [(sy, sx) for sx, sy in order]
    return [right[place] for place in order], [left[place] for place in order]


def final_kernel(*refs):
    buffers, total_ref, out_ref, l_top, totals, results, sem = (refs[:12], refs[12:24]), *refs[24:]
    tiles = [find_tiles(colour) for colour in range(2)]

    def columns_of(step):
        n = lax.rem(step, STEPS)
        return lax.div(step, STEPS), pl.ds(pl.multiple_of(n * CHUNK * 128, CHUNK * 128), CHUNK * 128)

    def fetch(step):
        q, cols = columns_of(step)
        slot = lax.rem(step, 2)
        return pltpu.make_async_copy(total_ref.at[q, :, cols], totals.at[slot], sem.at[slot])

    def store(step):
        q, cols = columns_of(step)
        slot = lax.rem(step, 2)
        return pltpu.make_async_copy(results.at[slot], out_ref.at[q, :, cols], sem.at[2 + slot])

    for step in range(2):
        fetch(step).start()
    metas = []
    for halves in tiles[0][0]:
        which, first = halves[1]
        metas.append(buffers[0][which][first + TILE_META - HALF])
    mine = jnp.concatenate(metas, axis=0)
    weight, key = mine[:, 0:1], mine[:, 1:2]
    diag = iota((128, 128), 0) == iota((128, 128), 1)
    key_row = jnp.sum(jnp.where(diag, key, 0.0), axis=0, keepdims=True)
    weight_row = jnp.sum(jnp.where(diag, weight, 0.0), axis=0, keepdims=True)
    own = jnp.sum(jnp.where(key == key_row, weight_row, 0.0), axis=1, keepdims=True)
    factors = weight / own
    for q in range(GQ):
        colour, k = q // 2, q % 2
        left = jnp.concatenate([buffers[colour][which][first + k] for which, first in tiles[colour][1]], axis=0)
        hi, lo = split2((left * factors).T)
        l_top[q] = jnp.concatenate([hi, lo, hi], axis=1)

    for q in range(GQ):
        places = [halves[q % 2] for halves in tiles[q // 2][0]]

        def body(n, carry):
            step = q * STEPS + n
            slot = lax.rem(step, 2)
            fetch(step).wait()

            @pl.when(step >= 2)
            def _():
                store(step).wait()

            left3 = l_top[q]
            for j in range(0, CHUNK, 2):
                right = jnp.concatenate(
                    [
                        jnp.concatenate(
                            [buffers[q // 2][which][first + n * CHUNK + j + k] for which, first in places], axis=0
                        )
                        for k in range(2)
                    ],
                    axis=1,
                )
                hi, lo = split2(right)
                right3 = jnp.concatenate([hi, hi, lo], axis=0)
                cols = slice(j * 128, (j + 2) * 128)
                results[slot, :, cols] = totals[slot, :, cols] + mm(left3, right3)
            store(step).start()

            @pl.when(step + 2 < GQ * STEPS)
            def _():
                fetch(step + 2).start()

            return carry

        lax.fori_loop(0, STEPS, body, 0)
    for slot in range(2):
        store(slot).wait()


ANY = pl.BlockSpec(memory_space=pl.ANY)
VMEM = pl.BlockSpec(memory_space=pltpu.VMEM)
SMEM = pl.BlockSpec(memory_space=pltpu.SMEM)


def sds(*shape):
    return jax.ShapeDtypeStruct(shape, F32)


UP = [(i, (i + 1) % 4) for i in range(4)]
DOWN = [(i, (i - 1) % 4) for i in range(4)]


def hop(axis, way, value):
    return lax.ppermute(value, axis, way)


def gather_planes(colours):
    axes = (("x", "y"), ("y", "x"))
    state = []
    for (first, _), (up, down, own) in zip(axes, colours):
        state.append([up, own, hop(first, UP, up), hop(first, DOWN, down)])
    for (first, _), found, size in zip(axes, state, (65, 64)):
        a, b = found[2], found[3]
        found.append(hop(first, UP, jnp.concatenate([a[:HALF], a[size + 8 :]], axis=0)))
        found.append(hop(first, DOWN, jnp.concatenate([b[HALF:size], b[size + 8 :]], axis=0)))
    for (_, second), found, size in zip(axes, state, (65, 64)):
        line = jnp.concatenate([found[0][:size], found[2][:size], found[3][:size]], axis=0)
        found.append(hop(second, UP, line))
        found.append(hop(second, DOWN, line))
    for (_, second), found, size in zip(axes, state, (65, 64)):
        _, own, a, b, c, d = found[:6]
        n = size
        opposite = [c[:HALF], d[: n - HALF]]
        up = [own[2:4], a[n + 2 : n + 4], b[n + 2 : n + 4], c[HALF + 2 : HALF + 4], own[4:6], a[n + 4 : n + 6]]
        down = [own[6:8], a[n + 6 : n + 8], b[n + 6 : n + 8], d[n - HALF + 2 :], b[n + 4 : n + 6], d[n - HALF : n - HALF + 2]]
        found.append(hop(second, UP, jnp.concatenate(opposite + up, axis=0)))
        found.append(hop(second, DOWN, jnp.concatenate(opposite + down, axis=0)))
    for (_, second), found, n in zip(axes, state, (65, 64)):
        e, f, g, h = found[6:10]
        cut = n + HALF
        found.append(hop(second, UP, jnp.concatenate([e[:cut], g[:HALF], g[n + 8 :]], axis=0)))
        found.append(hop(second, DOWN, jnp.concatenate([f[cut:], h[HALF:n], h[n + 8 :]], axis=0)))
    return state


def per_device(perturb, touched, spins, accept, site_ids, time_ids, left_proj, right_proj, weights, routing, total):
    blocks = pl.pallas_call(
        measure_kernel,
        out_shape=[sds(BLOCK_ROWS, 128)] * 8,
        in_specs=[VMEM] * 7 + [SMEM, SMEM, ANY],
        out_specs=[VMEM] * 8,
        scratch_shapes=[
            pltpu.VMEM((K, K), F32),
            pltpu.VMEM((K, K), BF16),
            pltpu.VMEM((K, K), BF16),
            pltpu.VMEM((LEG, K), F32),
            pltpu.VMEM((LEG * Q, K), F32),
            pltpu.VMEM((2, Q, K), F32),
            pltpu.VMEM((Q * 32, 128), F32),
            pltpu.VMEM((Q * 32, 128), F32),
            pltpu.SemaphoreType.DMA,
        ],
        compiler_params=pltpu.CompilerParams(vmem_limit_bytes=56 * MIB),
        name="measure",
    )(touched, spins, accept, site_ids, time_ids, left_proj, right_proj, weights, routing, perturb)
    here = [blocks[0]] + [
        lax.ppermute(blocks[d], ("zh", "c", "zl"), [(i, i ^ d) for i in range(8)]) for d in range(1, 8)
    ]
    packed = pl.pallas_call(
        assemble_kernel,
        out_shape=[sds(77, 8, 128), sds(77, 8, 128), sds(8, 8, 128), sds(76, 8, 128), sds(76, 8, 128), sds(8, 8, 128)],
        in_specs=[VMEM] * 8,
        out_specs=[VMEM] * 6,
        name="assemble",
    )(*here)
    one, two = gather_planes((packed[:3], packed[3:]))
    return pl.pallas_call(
        final_kernel,
        out_shape=sds(GQ, 128, SITES * LEG),
        in_specs=[VMEM] * 24 + [ANY],
        out_specs=ANY,
        scratch_shapes=[
            pltpu.VMEM((GQ, 128, 384), BF16),
            pltpu.VMEM((2, 128, CHUNK * 128), F32),
            pltpu.VMEM((2, 128, CHUNK * 128), F32),
            pltpu.SemaphoreType.DMA((4,)),
        ],
        compiler_params=pltpu.CompilerParams(vmem_limit_bytes=30 * MIB),
        name="accumulate",
    )(*one, *two, total)


def solution(mesh):
    cube = Mesh(mesh.devices.reshape(2, 2, 4, 4, 2), ("zh", "c", "x", "y", "zl"))
    grp, mem = ("zh", "c"), ("x", "y", "zl")
    both = grp + mem
    in_specs = (
        P(both, None, None),
        P(both, None, None),
        P(both, None, None),
        P(both, None, None),
        P(both, None),
        P(both, None),
        P(),
        P(),
        P(both),
        P(both, None),
        P(grp, mem, None),
    )
    return jax.shard_map(per_device, mesh=cube, in_specs=in_specs, out_specs=P(grp, mem, None), check_vma=False)
```

time: 145 us -> 131 us (0.903)
  waiting for transfers between devices: 50.8 us -> 65.8 us
  starting transfers between devices: 48.9 us -> 34.5 us
  Pallas kernels: 35.8 us -> 24.9 us
  local copies, waits for them, and re-layouts: 5.29 us -> 3.07 us
    ppermute x36 -> x20, waiting for transfers between devices: 43.9 us -> 58.4 us  [hop(): return lax.ppermute(value, axis, way)]
    ppermute x36 -> x20, starting transfers between devices: 38.5 us -> 24.1 us  [hop(): return lax.ppermute(value, axis, way)]
    pallas_call x2, Pallas kernels: 20.8 us -> 12.8 us  [the longest x1 9.77 us: per_device(): pl.pallas_call(final_kernel, out_shape=sds(GQ, 128, SITES * LEG), in_spec...]
    pallas_call x1, Pallas kernels: 15 us -> 12.1 us  [per_device(): pl.pallas_call(measure_kernel, out_shape=[sds(BLOCK_ROWS, 128)] * 8, in_s...]
    reshape x2 -> x0, local copies, waits for them, and re-layouts: 1.98 us -> none  [the longest x1 1.33 us: per_device(): chosen = touched.reshape(1, NS)]
    unnamed x18 -> x48, local copies, waits for them, and re-layouts: 2.52 us -> 0.8 us
    slice x4 -> x26, local copies, waits for them, and re-layouts: 0.79 us -> 2.25 us  [the longest x2 1.97 us: gather_planes(): found[0][:size]]
  transfers between devices with their start and end apart: 43 -> 27, of which waited for: 19 -> 13; matrix products, arithmetic and copies ran while one was open for 1% -> 2% of each run, Pallas kernels for 0% -> 0%
where the time goes in v2:
time: 131 us
  waiting for transfers between devices  65.8 us (50%)
  starting transfers between devices  34.5 us (26%)
  Pallas kernels  24.9 us (19%)
  local copies, waits for them, and re-layouts  3.07 us (2%)
  between operations  2.06 us (2%)
    ppermute x20, waiting for transfers between devices, hop(): return lax.ppermute(value, axis, way)  58.4 us
    ppermute x20, starting transfers between devices, hop(): return lax.ppermute(value, axis, way)  24.1 us
    pallas_call x1, Pallas kernels, per_device(): pl.pallas_call(measure_kernel, out_shape=[sds(BLOCK_ROWS, 128)] * 8, in_s...  12.1 us
    ppermute x7, starting transfers between devices, per_device(): lax.ppermute(blocks[d], ('zh', 'c', 'zl'), [(i, i ^ d) for i in range(8)])  10.4 us
    pallas_call x1, Pallas kernels, per_device(): pl.pallas_call(final_kernel, out_shape=sds(GQ, 128, SITES * LEG), in_spec...  9.77 us
    ppermute x7, waiting for transfers between devices, per_device(): lax.ppermute(blocks[d], ('zh', 'c', 'zl'), [(i, i ^ d) for i in range(8)])  7.46 us
    pallas_call x1, Pallas kernels, per_device(): pl.pallas_call(assemble_kernel, out_shape=[sds(77, 8, 128), sds(77, 8, 12...  3.02 us
  transfers between devices with their start and end apart: 27, of which 13 were waited for; matrix products, arithmetic and copies ran while one was open for 2% of the time, Pallas kernels for 0%

profile of v2, /device:TPU:0, one launch (start us, length us, event | category | flops | bytes accessed | tf_op | source)
XLA Modules:
  0.0 130.6 jit_solution(9925721871301376044)
XLA Ops:
  1.3 12.1 %measure.1 = (f32[200,128]{1,0:T(8,128)}, f32[200,128]{1,0:T(8,128)}, f32[200,128]{1,0:T(8,128)}, f32[200,128]{1,0:T(8,128)}, f32[200,128]{1,0:T(8,128)}, /*inde...) custom-call(s32[1,4,64]{2,1,0:T(4,128)} %chosen_ref.1, s32[1,4,64]{2,1,0:T(4,128)} %spin_ref.1, ...), custom_call_target="tpu_custom_call" | custom-call | tf_op jit(solution)/shard_map/measure/pallas_call | solution.py:382
  13.4 2.1 %collective-permute-start = (f32[200,128]{1,0:T(8,128)}, f32[200,128]{1,0:T(8,128)S(1)}, u32[]{:S(2)}, u32[]{:S(2)}) collective-permute-start(f32[200,128]{1,0:T(8,128)} %get-tuple-element.20), channel_id=1, source_target_pairs={{0,1},{1,0},{32,33},{33,32},{64,65},{65,64},{96,97},{97,96},{2,3},... | collective-permute-start | bytes 307208 | tf_op jit(solution)/shard_map/ppermute | solution.py:402
  15.5 0.0 collective-permute-start.1
  15.5 0.2 collective-permute-start.2
  15.7 3.9 %collective-permute-start.3 = (f32[200,128]{1,0:T(8,128)}, f32[200,128]{1,0:T(8,128)S(1)}, u32[]{:S(2)}, u32[]{:S(2)}) collective-permute-start(f32[200,128]{1,0:T(8,128)} %get-tuple-element.23), channel_id=1, source_target_pairs={{0,64},{1,65},{32,96},{33,97},{64,0},{65,1},{96,32},{97,33},{2,66}... | collective-permute-start | bytes 307208 | tf_op jit(solution)/shard_map/ppermute | solution.py:402
  19.6 0.7 collective-permute-start.4
  20.3 0.0 collective-permute-done.refs_1_
  20.3 1.4 %collective-permute-start.5 = (f32[200,128]{1,0:T(8,128)}, f32[200,128]{1,0:T(8,128)S(1)}, u32[]{:S(2)}, u32[]{:S(2)}) collective-permute-start(f32[200,128]{1,0:T(8,128)} %get-tuple-element.25), channel_id=1, source_target_pairs={{0,96},{1,97},{32,64},{33,65},{64,32},{65,33},{96,0},{97,1},{2,98}... | collective-permute-start | bytes 307208 | tf_op jit(solution)/shard_map/ppermute | solution.py:402
  21.7 0.0 collective-permute-done.1.refs_2_
  21.7 2.1 %collective-permute-start.6 = (f32[200,128]{1,0:T(8,128)}, f32[200,128]{1,0:T(8,128)S(1)}, u32[]{:S(2)}, u32[]{:S(2)}) collective-permute-start(f32[200,128]{1,0:T(8,128)} %get-tuple-element.26), channel_id=1, source_target_pairs={{0,97},{1,96},{32,65},{33,64},{64,33},{65,32},{96,1},{97,0},{2,99}... | collective-permute-start | bytes 307208 | tf_op jit(solution)/shard_map/ppermute | solution.py:402
  23.8 0.0 collective-permute-done.2.refs_3_
  23.8 3.6 %collective-permute-done.3.refs_4_ = f32[200,128]{1,0:T(8,128)S(1)} collective-permute-done((f32[200,128]{1,0:T(8,128)}, f32[200,128]{1,0:T(8,128)S(1)}, u32[]{:S(2)}, u32[]{:S(2)}) %collective-permute-start.3) | collective-permute-done | bytes 102432 | tf_op jit(solution)/shard_map/ppermute | solution.py:402
  27.5 2.9 %collective-permute-done.4.refs_5_ = f32[200,128]{1,0:T(8,128)S(1)} collective-permute-done((f32[200,128]{1,0:T(8,128)}, f32[200,128]{1,0:T(8,128)S(1)}, u32[]{:S(2)}, u32[]{:S(2)}) %collective-permute-start.4) | collective-permute-done | bytes 102432 | tf_op jit(solution)/shard_map/ppermute | solution.py:402
  30.3 0.0 collective-permute-done.5.refs_6_
  30.4 0.9 collective-permute-done.6.refs_7_
  31.3 0.6 copy-done.10
  31.9 3.0 %assemble.1 = (f32[77,8,128]{2,1,0:T(8,128)}, f32[77,8,128]{2,1,0:T(8,128)}, f32[8,8,128]{2,1,0:T(8,128)}, f32[76,8,128]{2,1,0:T(8,128)}, f32[76,8,128]{2,1,0:T(8,128)}, /*index=5*/f32[8,8,128]{2,1,0:T(8,128)}) custom-call(f32[200,128]{1,0:T(8,128)} %get-tuple-element.19.refs_0_, f32[200,128]{1,0:T(8,128)} %copy-done.4, f32[200,128]{1,0:T(8,128)} %copy-done.5, ...), custom_call_target="tpu_custom_call" | custom-call | tf_op jit(solution)/shard_map/assemble/pallas_call | solution.py:404
  35.0 3.1 %collective-permute-start.18 = (f32[76,8,128]{2,1,0:T(8,128)}, f32[76,8,128]{2,1,0:T(8,128)S(1)}, u32[]{:S(2)}, u32[]{:S(2)}) collective-permute-start(f32[76,8,128]{2,1,0:T(8,128)} %get-tuple-element.32), channel_id=1, source_target_pairs={{0,6},{2,0},{4,2},{6,4},{1,7},{3,1},{5,3},{7,5},{8,14},{10,8},{12,... | collective-permute-start | bytes 933896 | tf_op jit(solution)/shard_map/ppermute | solution.py:349
  38.1 0.0 collective-permute-start.17
  38.1 1.0 slice.193
  39.1 1.0 slice.166
  40.0 1.6 %collective-permute-start.7 = (f32[77,8,128]{2,1,0:T(8,128)}, f32[77,8,128]{2,1,0:T(8,128)S(1)}, u32[]{:S(2)}, u32[]{:S(2)}) collective-permute-start(f32[77,8,128]{2,1,0:T(8,128)} %get-tuple-element.27.refs_0_), channel_id=1, source_target_pairs={{0,8},{8,16},{16,24},{24,0},{1,9},{9,17},{17,25},{25,1},{2,10},{10... | collective-permute-start | bytes 946184 | tf_op jit(solution)/shard_map/ppermute | solution.py:349
  41.6 1.7 %collective-permute-start.8 = (f32[77,8,128]{2,1,0:T(8,128)}, f32[77,8,128]{2,1,0:T(8,128)S(1)}, u32[]{:S(2)}, u32[]{:S(2)}) collective-permute-start(f32[77,8,128]{2,1,0:T(8,128)} %get-tuple-element.29), channel_id=1, source_target_pairs={{0,24},{8,0},{16,8},{24,16},{1,25},{9,1},{17,9},{25,17},{2,26},{10... | collective-permute-start | bytes 946184 | tf_op jit(solution)/shard_map/ppermute | solution.py:349
  43.3 2.3 %collective-permute-done.18.refs_15_ = f32[76,8,128]{2,1,0:T(8,128)S(1)} collective-permute-done((f32[76,8,128]{2,1,0:T(8,128)}, f32[76,8,128]{2,1,0:T(8,128)S(1)}, u32[]{:S(2)}, u32[]{:S(2)}) %collective-permute-start.18) | collective-permute-done | bytes 311328 | tf_op jit(solution)/shard_map/ppermute | solution.py:349
  45.6 3.3 %collective-permute-done.17.refs_14_ = f32[76,8,128]{2,1,0:T(8,128)S(1)} collective-permute-done((f32[76,8,128]{2,1,0:T(8,128)}, f32[76,8,128]{2,1,0:T(8,128)S(1)}, u32[]{:S(2)}, u32[]{:S(2)}) %collective-permute-start.17) | collective-permute-done | bytes 311328 | tf_op jit(solution)/shard_map/ppermute | solution.py:349
  48.9 0.1 pad_maximum_fusion.1
  49.0 0.0 slice-start
  49.0 0.0 copy-start
  49.0 3.0 %collective-permute-start.22 = (f32[192,8,128]{2,1,0:T(8,128)S(1)}, f32[192,8,128]{2,1,0:T(8,128)S(1)}, u32[]{:S(2)}, u32[]{:S(2)}) collective-permute-start(f32[192,8,128]{2,1,0:T(8,128)S(1)} %pad_maximum_fusion.1), channel_id=1, source_target_pairs={{0,24},{8,0},{16,8},{24,16},{1,25},{9,1},{17,9},{25,17},{2,26},{10... | collective-permute-start | bytes 2359304 | tf_op jit(solution)/shard_map/ppermute | solution.py:349
  52.0 0.0 collective-permute-start.21
  52.1 0.4 collective-permute-start.20
  52.5 0.0 collective-permute-done.8.refs_3_
  52.5 1.8 %collective-permute-start.19 = (f32[36,8,128]{2,1,0:T(8,128)S(1)}, f32[36,8,128]{2,1,0:T(8,128)S(1)}, u32[]{:S(2)}, u32[]{:S(2)}) collective-permute-start(f32[36,8,128]{2,1,0:T(8,128)S(1)} %pad_maximum_fusion.8), channel_id=1, source_target_pairs={{0,2},{2,4},{4,6},{6,0},{1,3},{3,5},{5,7},{7,1},{8,10},{10,12},{12... | collective-permute-start | bytes 442376 | tf_op jit(solution)/shard_map/ppermute | solution.py:349
  54.3 0.0 collective-permute-done.7.refs_2_
  54.3 3.3 %collective-permute-start.10 = (f32[37,8,128]{2,1,0:T(8,128)S(1)}, f32[37,8,128]{2,1,0:T(8,128)S(1)}, u32[]{:S(2)}, u32[]{:S(2)}) collective-permute-start(f32[37,8,128]{2,1,0:T(8,128)S(1)} %pad_maximum_fusion.6), channel_id=1, source_target_pairs={{0,24},{8,0},{16,8},{24,16},{1,25},{9,1},{17,9},{25,17},{2,26},{10... | collective-permute-start | bytes 454664 | tf_op jit(solution)/shard_map/ppermute | solution.py:349
  57.7 0.1 pad_maximum_fusion
  57.8 1.1 collective-permute-done.19.refs_16_
  58.9 1.0 collective-permute-start.9
  60.0 0.0 collective-permute-done.20.refs_17_
  60.0 2.1 %collective-permute-start.12 = (f32[195,8,128]{2,1,0:T(8,128)S(1)}, f32[195,8,128]{2,1,0:T(8,128)S(1)}, u32[]{:S(2)}, u32[]{:S(2)}) collective-permute-start(f32[195,8,128]{2,1,0:T(8,128)S(1)} %pad_maximum_fusion), channel_id=1, source_target_pairs={{0,6},{2,0},{4,2},{6,4},{1,7},{3,1},{5,3},{7,5},{8,14},{10,8},{12,... | collective-permute-start | bytes 2396168 | tf_op jit(solution)/shard_map/ppermute | solution.py:349
  62.2 12.6 %collective-permute-done.9.refs_4_ = f32[36,8,128]{2,1,0:T(8,128)S(1)} collective-permute-done((f32[36,8,128]{2,1,0:T(8,128)S(1)}, f32[36,8,128]{2,1,0:T(8,128)S(1)}, u32[]{:S(2)}, u32[]{:S(2)}) %collective-permute-start.9) | collective-permute-done | bytes 147488 | tf_op jit(solution)/shard_map/ppermute | solution.py:349
  74.9 0.0 collective-permute-start.23
  74.9 0.0 collective-permute-done.10.refs_5_
  74.9 3.3 %collective-permute-start.24 = (f32[76,8,128]{2,1,0:T(8,128)S(1)}, f32[76,8,128]{2,1,0:T(8,128)S(1)}, u32[]{:S(2)}, u32[]{:S(2)}) collective-permute-start(f32[76,8,128]{2,1,0:T(8,128)S(1)} %constant_dynamic-update-slice_fusion.18), channel_id=1, source_target_pairs={{0,24},{8,0},{16,8},{24,16},{1,25},{9,1},{17,9},{25,17},{2,26},{10... | collective-permute-start | bytes 933896 | tf_op jit(solution)/shard_map/ppermute | solution.py:349
  78.4 5.2 %collective-permute-done.23.refs_20_ = f32[76,8,128]{2,1,0:T(8,128)S(1)} collective-permute-done((f32[76,8,128]{2,1,0:T(8,128)S(1)}, f32[76,8,128]{2,1,0:T(8,128)S(1)}, u32[]{:S(2)}, u32[]{:S(2)}) %collective-permute-start.23) | collective-permute-done | bytes 311328 | tf_op jit(solution)/shard_map/ppermute | solution.py:349
  83.5 0.0 collective-permute-start.13
  83.5 0.0 collective-permute-done.24.refs_21_
  83.5 0.0 collective-permute-start.11
  83.6 11.5 %collective-permute-done.13.refs_8_ = f32[77,8,128]{2,1,0:T(8,128)S(1)} collective-permute-done((f32[77,8,128]{2,1,0:T(8,128)S(1)}, f32[77,8,128]{2,1,0:T(8,128)S(1)}, u32[]{:S(2)}, u32[]{:S(2)}) %collective-permute-start.13) | collective-permute-done | bytes 315424 | tf_op jit(solution)/shard_map/ppermute | solution.py:349
  95.1 0.0 collective-permute-start.14
  95.1 0.0 slice-start.1
  95.1 10.2 %collective-permute-done.14.refs_9_ = f32[77,8,128]{2,1,0:T(8,128)S(1)} collective-permute-done((f32[77,8,128]{2,1,0:T(8,128)S(1)}, f32[77,8,128]{2,1,0:T(8,128)S(1)}, u32[]{:S(2)}, u32[]{:S(2)}) %collective-permute-start.14) | collective-permute-done | bytes 315424 | tf_op jit(solution)/shard_map/ppermute | solution.py:349
  105.4 0.0 collective-permute-done.22.refs_19_
  105.5 0.1 collective-permute-start.26
  105.6 0.0 collective-permute-done.12.refs_7_
  105.7 1.3 collective-permute-start.16
  107.0 1.5 %collective-permute-done.11.refs_6_ = f32[195,8,128]{2,1,0:T(8,128)S(1)} collective-permute-done((f32[195,8,128]{2,1,0:T(8,128)S(1)}, f32[195,8,128]{2,1,0:T(8,128)S(1)}, u32[]{:S(2)}, u32[]{:S(2)}) %collective-permute-start.11) | collective-permute-done | bytes 798752 | tf_op jit(solution)/shard_map/ppermute | solution.py:349
  108.6 0.1 collective-permute-start.15
  108.7 1.3 %collective-permute-start.25 = (f32[132,8,128]{2,1,0:T(8,128)S(1)}, f32[132,8,128]{2,1,0:T(8,128)S(1)}, u32[]{:S(2)}, u32[]{:S(2)}) collective-permute-start(f32[132,8,128]{2,1,0:T(8,128)S(1)} %pad_maximum_fusion.4), channel_id=1, source_target_pairs={{0,8},{8,16},{16,24},{24,0},{1,9},{9,17},{17,25},{25,1},{2,10},{10... | collective-permute-start | bytes 1622024 | tf_op jit(solution)/shard_map/ppermute | solution.py:349
  110.1 4.9 %collective-permute-done.26.refs_23_ = f32[132,8,128]{2,1,0:T(8,128)S(1)} collective-permute-done((f32[132,8,128]{2,1,0:T(8,128)S(1)}, f32[132,8,128]{2,1,0:T(8,128)S(1)}, u32[]{:S(2)}, u32[]{:S(2)}) %collective-permute-start.26) | collective-permute-done | bytes 540704 | tf_op jit(solution)/shard_map/ppermute | solution.py:349
  114.9 5.7 %collective-permute-done.25.refs_22_ = f32[132,8,128]{2,1,0:T(8,128)S(1)} collective-permute-done((f32[132,8,128]{2,1,0:T(8,128)S(1)}, f32[132,8,128]{2,1,0:T(8,128)S(1)}, u32[]{:S(2)}, u32[]{:S(2)}) %collective-permute-start.25) | collective-permute-done | bytes 540704 | tf_op jit(solution)/shard_map/ppermute | solution.py:349
  120.6 0.0 collective-permute-done.15.refs_10_
  120.7 0.0 collective-permute-done.16.refs_11_
  120.7 9.8 %accumulate.1 = f32[4,128,4096]{2,1,0:T(8,128)} custom-call(f32[77,8,128]{2,1,0:T(8,128)S(1)} %copy-done, f32[8,8,128]{2,1,0:T(8,128)S(1)} %copy-done.2, f32[77,8,128]{2,1,0:T(8,128)S(1)} %collective-permute-done.7.refs_2_, f32[77,8,128]{2,1,0:T(8,128)S(1)} %collective-permute-done.8.refs_3_, f32[36,8,128]{2,1,0:T(8,128)S(1)} %collective-permute-done.9.refs_4_, ...), custom_call_target="tpu_custom_call" | custom-call | tf_op jit(solution)/shard_map/accumulate/pallas_call | solution.py:412
  (82 shorter events, 0.7 us)
Async XLA Ops:
  13.4 6.9 %collective-permute-start = (f32[200,128]{1,0:T(8,128)}, f32[200,128]{1,0:T(8,128)S(1)}, u32[]{:S(2)}, u32[]{:S(2)}) collective-permute-start(f32[200,128]{1,0:T(8,128)} %get-tuple-element.20), channel_id=1, source_target_pairs={{0,1},{1,0},{32,33},{33,32},{64,65},{65,64},{96,97},{97,96},{2,3},... | collective-permute-start | bytes 307208 | tf_op jit(solution)/shard_map/ppermute | solution.py:402
  15.5 6.2 %collective-permute-start.1 = (f32[200,128]{1,0:T(8,128)}, f32[200,128]{1,0:T(8,128)S(1)}, u32[]{:S(2)}, u32[]{:S(2)}) collective-permute-start(f32[200,128]{1,0:T(8,128)} %get-tuple-element.21), channel_id=1, source_target_pairs={{0,32},{1,33},{32,0},{33,1},{64,96},{65,97},{96,64},{97,65},{2,34}... | collective-permute-start | bytes 307208 | tf_op jit(solution)/shard_map/ppermute | solution.py:402
  15.5 8.3 %collective-permute-start.2 = (f32[200,128]{1,0:T(8,128)}, f32[200,128]{1,0:T(8,128)S(1)}, u32[]{:S(2)}, u32[]{:S(2)}) collective-permute-start(f32[200,128]{1,0:T(8,128)} %get-tuple-element.22), channel_id=1, source_target_pairs={{0,33},{1,32},{32,1},{33,0},{64,97},{65,96},{96,65},{97,64},{2,35}... | collective-permute-start | bytes 307208 | tf_op jit(solution)/shard_map/ppermute | solution.py:402
  15.7 11.8 %collective-permute-start.3 = (f32[200,128]{1,0:T(8,128)}, f32[200,128]{1,0:T(8,128)S(1)}, u32[]{:S(2)}, u32[]{:S(2)}) collective-permute-start(f32[200,128]{1,0:T(8,128)} %get-tuple-element.23), channel_id=1, source_target_pairs={{0,64},{1,65},{32,96},{33,97},{64,0},{65,1},{96,32},{97,33},{2,66}... | collective-permute-start | bytes 307208 | tf_op jit(solution)/shard_map/ppermute | solution.py:402
  19.6 10.7 %collective-permute-start.4 = (f32[200,128]{1,0:T(8,128)}, f32[200,128]{1,0:T(8,128)S(1)}, u32[]{:S(2)}, u32[]{:S(2)}) collective-permute-start(f32[200,128]{1,0:T(8,128)} %get-tuple-element.24), channel_id=1, source_target_pairs={{0,65},{1,64},{32,97},{33,96},{64,1},{65,0},{96,33},{97,32},{2,67}... | collective-permute-start | bytes 307208 | tf_op jit(solution)/shard_map/ppermute | solution.py:402
  20.3 11.0 %copy-start.4 = (f32[200,128]{1,0:T(8,128)}, f32[200,128]{1,0:T(8,128)S(1)}, u32[]{:S(2)}) copy-start(f32[200,128]{1,0:T(8,128)S(1)} %collective-permute-done.refs_1_) | copy-start | bytes 307204
  20.3 10.0 %collective-permute-start.5 = (f32[200,128]{1,0:T(8,128)}, f32[200,128]{1,0:T(8,128)S(1)}, u32[]{:S(2)}, u32[]{:S(2)}) collective-permute-start(f32[200,128]{1,0:T(8,128)} %get-tuple-element.25), channel_id=1, source_target_pairs={{0,96},{1,97},{32,64},{33,65},{64,32},{65,33},{96,0},{97,1},{2,98}... | collective-permute-start | bytes 307208 | tf_op jit(solution)/shard_map/ppermute | solution.py:402
  21.7 9.6 %copy-start.5 = (f32[200,128]{1,0:T(8,128)}, f32[200,128]{1,0:T(8,128)S(1)}, u32[]{:S(2)}) copy-start(f32[200,128]{1,0:T(8,128)S(1)} %collective-permute-done.1.refs_2_) | copy-start | bytes 307204
  21.7 9.6 %collective-permute-start.6 = (f32[200,128]{1,0:T(8,128)}, f32[200,128]{1,0:T(8,128)S(1)}, u32[]{:S(2)}, u32[]{:S(2)}) collective-permute-start(f32[200,128]{1,0:T(8,128)} %get-tuple-element.26), channel_id=1, source_target_pairs={{0,97},{1,96},{32,65},{33,64},{64,33},{65,32},{96,1},{97,0},{2,99}... | collective-permute-start | bytes 307208 | tf_op jit(solution)/shard_map/ppermute | solution.py:402
  23.8 7.5 %copy-start.6 = (f32[200,128]{1,0:T(8,128)}, f32[200,128]{1,0:T(8,128)S(1)}, u32[]{:S(2)}) copy-start(f32[200,128]{1,0:T(8,128)S(1)} %collective-permute-done.2.refs_3_) | copy-start | bytes 307204
  27.5 3.8 %copy-start.7 = (f32[200,128]{1,0:T(8,128)}, f32[200,128]{1,0:T(8,128)S(1)}, u32[]{:S(2)}) copy-start(f32[200,128]{1,0:T(8,128)S(1)} %collective-permute-done.3.refs_4_) | copy-start | bytes 307204
  30.3 1.0 copy-start.8
  30.3 1.0 copy-start.9
  31.3 0.7 copy-start.10
  35.0 27.2 %copy-start.3 = (f32[8,8,128]{2,1,0:T(8,128)S(1)}, f32[8,8,128]{2,1,0:T(8,128)}, u32[]{:S(2)}) copy-start(f32[8,8,128]{2,1,0:T(8,128)} %get-tuple-element.31.refs_13_) | copy-start | bytes 98308
  35.0 43.3 %copy-start.2 = (f32[8,8,128]{2,1,0:T(8,128)S(1)}, f32[8,8,128]{2,1,0:T(8,128)}, u32[]{:S(2)}) copy-start(f32[8,8,128]{2,1,0:T(8,128)} %get-tuple-element.28.refs_1_) | copy-start | bytes 98308
  35.0 10.6 %collective-permute-start.18 = (f32[76,8,128]{2,1,0:T(8,128)}, f32[76,8,128]{2,1,0:T(8,128)S(1)}, u32[]{:S(2)}, u32[]{:S(2)}) collective-permute-start(f32[76,8,128]{2,1,0:T(8,128)} %get-tuple-element.32), channel_id=1, source_target_pairs={{0,6},{2,0},{4,2},{6,4},{1,7},{3,1},{5,3},{7,5},{8,14},{10,8},{12,... | collective-permute-start | bytes 933896 | tf_op jit(solution)/shard_map/ppermute | solution.py:349
  38.1 10.9 %collective-permute-start.17 = (f32[76,8,128]{2,1,0:T(8,128)}, f32[76,8,128]{2,1,0:T(8,128)S(1)}, u32[]{:S(2)}, u32[]{:S(2)}) collective-permute-start(f32[76,8,128]{2,1,0:T(8,128)} %get-tuple-element.30.refs_12_), channel_id=1, source_target_pairs={{0,2},{2,4},{4,6},{6,0},{1,3},{3,5},{5,7},{7,1},{8,10},{10,12},{12... | collective-permute-start | bytes 933896 | tf_op jit(solution)/shard_map/ppermute | solution.py:349
  40.0 14.3 %collective-permute-start.7 = (f32[77,8,128]{2,1,0:T(8,128)}, f32[77,8,128]{2,1,0:T(8,128)S(1)}, u32[]{:S(2)}, u32[]{:S(2)}) collective-permute-start(f32[77,8,128]{2,1,0:T(8,128)} %get-tuple-element.27.refs_0_), channel_id=1, source_target_pairs={{0,8},{8,16},{16,24},{24,0},{1,9},{9,17},{17,25},{25,1},{2,10},{10... | collective-permute-start | bytes 946184 | tf_op jit(solution)/shard_map/ppermute | solution.py:349
  41.6 10.9 %collective-permute-start.8 = (f32[77,8,128]{2,1,0:T(8,128)}, f32[77,8,128]{2,1,0:T(8,128)S(1)}, u32[]{:S(2)}, u32[]{:S(2)}) collective-permute-start(f32[77,8,128]{2,1,0:T(8,128)} %get-tuple-element.29), channel_id=1, source_target_pairs={{0,24},{8,0},{16,8},{24,16},{1,25},{9,1},{17,9},{25,17},{2,26},{10... | collective-permute-start | bytes 946184 | tf_op jit(solution)/shard_map/ppermute | solution.py:349
  49.0 71.7 %slice-start = ((s8[8388608]{0:T(1024)(128)(4,1)}), s8[4194304]{0:T(1024)(128)(4,1)S(1)}, s32[]{:S(2)}) async-start(s8[8388608]{0:T(1024)(128)(4,1)} %bitcast), calls=%async_computation | async-start | bytes 8388608
  49.0 71.7 %copy-start = (f32[77,8,128]{2,1,0:T(8,128)S(1)}, f32[77,8,128]{2,1,0:T(8,128)}, u32[]{:S(2)}) copy-start(f32[77,8,128]{2,1,0:T(8,128)} %get-tuple-element.27.refs_0_) | copy-start | bytes 946180
  49.0 71.7 %copy-start.1 = (f32[76,8,128]{2,1,0:T(8,128)S(1)}, f32[76,8,128]{2,1,0:T(8,128)}, u32[]{:S(2)}) copy-start(f32[76,8,128]{2,1,0:T(8,128)} %get-tuple-element.30.refs_12_) | copy-start | bytes 933892
  49.0 56.4 %collective-permute-start.22 = (f32[192,8,128]{2,1,0:T(8,128)S(1)}, f32[192,8,128]{2,1,0:T(8,128)S(1)}, u32[]{:S(2)}, u32[]{:S(2)}) collective-permute-start(f32[192,8,128]{2,1,0:T(8,128)S(1)} %pad_maximum_fusion.1), channel_id=1, source_target_pairs={{0,24},{8,0},{16,8},{24,16},{1,25},{9,1},{17,9},{25,17},{2,26},{10... | collective-permute-start | bytes 2359304 | tf_op jit(solution)/shard_map/ppermute | solution.py:349
  52.0 53.5 %collective-permute-start.21 = (f32[192,8,128]{2,1,0:T(8,128)S(1)}, f32[192,8,128]{2,1,0:T(8,128)S(1)}, u32[]{:S(2)}, u32[]{:S(2)}) collective-permute-start(f32[192,8,128]{2,1,0:T(8,128)S(1)} %pad_maximum_fusion.1), channel_id=1, source_target_pairs={{0,8},{8,16},{16,24},{24,0},{1,9},{9,17},{17,25},{25,1},{2,10},{10... | collective-permute-start | bytes 2359304 | tf_op jit(solution)/shard_map/ppermute | solution.py:349
  52.1 7.9 %collective-permute-start.20 = (f32[36,8,128]{2,1,0:T(8,128)S(1)}, f32[36,8,128]{2,1,0:T(8,128)S(1)}, u32[]{:S(2)}, u32[]{:S(2)}) collective-permute-start(f32[36,8,128]{2,1,0:T(8,128)S(1)} %pad_maximum_fusion.9), channel_id=1, source_target_pairs={{0,6},{2,0},{4,2},{6,4},{1,7},{3,1},{5,3},{7,5},{8,14},{10,8},{12,... | collective-permute-start | bytes 442376 | tf_op jit(solution)/shard_map/ppermute | solution.py:349
  52.5 6.4 %collective-permute-start.19 = (f32[36,8,128]{2,1,0:T(8,128)S(1)}, f32[36,8,128]{2,1,0:T(8,128)S(1)}, u32[]{:S(2)}, u32[]{:S(2)}) collective-permute-start(f32[36,8,128]{2,1,0:T(8,128)S(1)} %pad_maximum_fusion.8), channel_id=1, source_target_pairs={{0,2},{2,4},{4,6},{6,0},{1,3},{3,5},{5,7},{7,1},{8,10},{10,12},{12... | collective-permute-start | bytes 442376 | tf_op jit(solution)/shard_map/ppermute | solution.py:349
  54.3 20.6 %collective-permute-start.10 = (f32[37,8,128]{2,1,0:T(8,128)S(1)}, f32[37,8,128]{2,1,0:T(8,128)S(1)}, u32[]{:S(2)}, u32[]{:S(2)}) collective-permute-start(f32[37,8,128]{2,1,0:T(8,128)S(1)} %pad_maximum_fusion.6), channel_id=1, source_target_pairs={{0,24},{8,0},{16,8},{24,16},{1,25},{9,1},{17,9},{25,17},{2,26},{10... | collective-permute-start | bytes 454664 | tf_op jit(solution)/shard_map/ppermute | solution.py:349
  58.9 16.0 %collective-permute-start.9 = (f32[36,8,128]{2,1,0:T(8,128)S(1)}, f32[36,8,128]{2,1,0:T(8,128)S(1)}, u32[]{:S(2)}, u32[]{:S(2)}) collective-permute-start(f32[36,8,128]{2,1,0:T(8,128)S(1)} %pad_maximum_fusion.7), channel_id=1, source_target_pairs={{0,8},{8,16},{16,24},{24,0},{1,9},{9,17},{17,25},{25,1},{2,10},{10... | collective-permute-start | bytes 442376 | tf_op jit(solution)/shard_map/ppermute | solution.py:349
  60.0 45.6 %collective-permute-start.12 = (f32[195,8,128]{2,1,0:T(8,128)S(1)}, f32[195,8,128]{2,1,0:T(8,128)S(1)}, u32[]{:S(2)}, u32[]{:S(2)}) collective-permute-start(f32[195,8,128]{2,1,0:T(8,128)S(1)} %pad_maximum_fusion), channel_id=1, source_target_pairs={{0,6},{2,0},{4,2},{6,4},{1,7},{3,1},{5,3},{7,5},{8,14},{10,8},{12,... | collective-permute-start | bytes 2396168 | tf_op jit(solution)/shard_map/ppermute | solution.py:349
  74.9 8.6 %collective-permute-start.23 = (f32[76,8,128]{2,1,0:T(8,128)S(1)}, f32[76,8,128]{2,1,0:T(8,128)S(1)}, u32[]{:S(2)}, u32[]{:S(2)}) collective-permute-start(f32[76,8,128]{2,1,0:T(8,128)S(1)} %constant_dynamic-update-slice_fusion.12), channel_id=1, source_target_pairs={{0,8},{8,16},{16,24},{24,0},{1,9},{9,17},{17,25},{25,1},{2,10},{10... | collective-permute-start | bytes 933896 | tf_op jit(solution)/shard_map/ppermute | solution.py:349
  74.9 8.6 %collective-permute-start.24 = (f32[76,8,128]{2,1,0:T(8,128)S(1)}, f32[76,8,128]{2,1,0:T(8,128)S(1)}, u32[]{:S(2)}, u32[]{:S(2)}) collective-permute-start(f32[76,8,128]{2,1,0:T(8,128)S(1)} %constant_dynamic-update-slice_fusion.18), channel_id=1, source_target_pairs={{0,24},{8,0},{16,8},{24,16},{1,25},{9,1},{17,9},{25,17},{2,26},{10... | collective-permute-start | bytes 933896 | tf_op jit(solution)/shard_map/ppermute | solution.py:349
  83.5 11.5 %collective-permute-start.13 = (f32[77,8,128]{2,1,0:T(8,128)S(1)}, f32[77,8,128]{2,1,0:T(8,128)S(1)}, u32[]{:S(2)}, u32[]{:S(2)}) collective-permute-start(f32[77,8,128]{2,1,0:T(8,128)S(1)} %constant_dynamic-update-slice_fusion), channel_id=1, source_target_pairs={{0,2},{2,4},{4,6},{6,0},{1,3},{3,5},{5,7},{7,1},{8,10},{10,12},{12... | collective-permute-start | bytes 946184 | tf_op jit(solution)/shard_map/ppermute | solution.py:349
  83.5 25.0 %collective-permute-start.11 = (f32[195,8,128]{2,1,0:T(8,128)S(1)}, f32[195,8,128]{2,1,0:T(8,128)S(1)}, u32[]{:S(2)}, u32[]{:S(2)}) collective-permute-start(f32[195,8,128]{2,1,0:T(8,128)S(1)} %pad_maximum_fusion), channel_id=1, source_target_pairs={{0,2},{2,4},{4,6},{6,0},{1,3},{3,5},{5,7},{7,1},{8,10},{10,12},{12... | collective-permute-start | bytes 2396168 | tf_op jit(solution)/shard_map/ppermute | solution.py:349
  95.1 10.3 %collective-permute-start.14 = (f32[77,8,128]{2,1,0:T(8,128)S(1)}, f32[77,8,128]{2,1,0:T(8,128)S(1)}, u32[]{:S(2)}, u32[]{:S(2)}) collective-permute-start(f32[77,8,128]{2,1,0:T(8,128)S(1)} %constant_dynamic-update-slice_fusion.6), channel_id=1, source_target_pairs={{0,6},{2,0},{4,2},{6,4},{1,7},{3,1},{5,3},{7,5},{8,14},{10,8},{12,... | collective-permute-start | bytes 946184 | tf_op jit(solution)/shard_map/ppermute | solution.py:349
  95.1 25.6 %slice-start.1 = ((s8[8388608]{0:T(1024)(128)(4,1)}), s8[4194304]{0:T(1024)(128)(4,1)S(1)}, s32[]{:S(2)}) async-start(s8[8388608]{0:T(1024)(128)(4,1)} %bitcast), calls=%async_computation.1 | async-start | bytes 8388608
  105.5 9.4 %collective-permute-start.26 = (f32[132,8,128]{2,1,0:T(8,128)S(1)}, f32[132,8,128]{2,1,0:T(8,128)S(1)}, u32[]{:S(2)}, u32[]{:S(2)}) collective-permute-start(f32[132,8,128]{2,1,0:T(8,128)S(1)} %pad_maximum_fusion.5), channel_id=1, source_target_pairs={{0,24},{8,0},{16,8},{24,16},{1,25},{9,1},{17,9},{25,17},{2,26},{10... | collective-permute-start | bytes 1622024 | tf_op jit(solution)/shard_map/ppermute | solution.py:349
  105.7 14.9 %collective-permute-start.16 = (f32[135,8,128]{2,1,0:T(8,128)S(1)}, f32[135,8,128]{2,1,0:T(8,128)S(1)}, u32[]{:S(2)}, u32[]{:S(2)}) collective-permute-start(f32[135,8,128]{2,1,0:T(8,128)S(1)} %pad_maximum_fusion.2), channel_id=1, source_target_pairs={{0,6},{2,0},{4,2},{6,4},{1,7},{3,1},{5,3},{7,5},{8,14},{10,8},{12,... | collective-permute-start | bytes 1658888 | tf_op jit(solution)/shard_map/ppermute | solution.py:349
  108.6 12.1 %collective-permute-start.15 = (f32[133,8,128]{2,1,0:T(8,128)S(1)}, f32[133,8,128]{2,1,0:T(8,128)S(1)}, u32[]{:S(2)}, u32[]{:S(2)}) collective-permute-start(f32[133,8,128]{2,1,0:T(8,128)S(1)} %pad_maximum_fusion.3), channel_id=1, source_target_pairs={{0,2},{2,4},{4,6},{6,0},{1,3},{3,5},{5,7},{7,1},{8,10},{10,12},{12... | collective-permute-start | bytes 1634312 | tf_op jit(solution)/shard_map/ppermute | solution.py:349
  108.7 11.9 %collective-permute-start.25 = (f32[132,8,128]{2,1,0:T(8,128)S(1)}, f32[132,8,128]{2,1,0:T(8,128)S(1)}, u32[]{:S(2)}, u32[]{:S(2)}) collective-permute-start(f32[132,8,128]{2,1,0:T(8,128)S(1)} %pad_maximum_fusion.4), channel_id=1, source_target_pairs={{0,8},{8,16},{16,24},{24,0},{1,9},{9,17},{17,25},{25,1},{2,10},{10... | collective-permute-start | bytes 1622024 | tf_op jit(solution)/shard_map/ppermute | solution.py:349

commit v3 on v2

--- a/solution.py
+++ b/solution.py
@@ -132,8 +132,10 @@
         if update < UPDATES - 1:
             c_all = c_all + columns
             r_all = jnp.where(row_block == update, rows_now, r_all)
+            half = slice(update // 2 * 128, update // 2 * 128 + 128)
+            columns, y_now, rows_now = columns[:, half], y_now[:, half], split2(rows_now[half])
             change = mm3(jnp.concatenate([columns, y_now], axis=0), rows_now)
-            p_vec = p_vec - mm3(columns, p_vec)
+            p_vec = p_vec - mm3(columns, p_vec[half])
             small = small - change[:NS]
             q_vec = q_vec - change[NS:]
     lower = split2(jnp.where(row_block > col_block, c_all, 0.0))
@@ -145,7 +147,10 @@
     y2 = y2 - mm3(y2, lower)
     zs, ys = split3(z * gamma_column), split3(y2)
     left_arg = v - (mm(zs[0], pick, TN) + mm(zs[1], pick, TN) + mm(zs[2], pick, TN))
-    left_image = v + mm3(left_arg, (ph, plo), NT)
+    ah, al = split2(left_arg)
+    streamed = mm(ph, jnp.concatenate([ah, al], axis=0), NT)
+    streamed = streamed[:, :Q] + (streamed[:, Q:] + mm(plo, ah, NT))
+    left_image = v + streamed.T
     right_arg = w - (mm(ys[0], pick) + mm(ys[1], pick) + mm(ys[2], pick))
     right_image = right_arg + from_w - mm3((ys[0], ys[1]), (rows_hi, rows_lo))
 
@@ -192,20 +197,18 @@
         size = 65 - colour
         for d in range(8):
             rows = blocks[d][colour * 64 : (colour + 1) * 64, :]
-            up[0:64, d, :] = rows
-            down[0:64, d, :] = rows
-            if colour == 0:
-                first = RIGHT_ROWS + LEFT_ROWS
-                up[TILE_META, d : d + 1, :] = blocks[d][first : first + 1, :]
-                down[TILE_META, d : d + 1, :] = blocks[d][first : first + 1, :]
+            for ref in (up, down):
+                ref[pl.ds(d, 64, stride=8), :] = rows
+                if colour == 0:
+                    first = RIGHT_ROWS + LEFT_ROWS
+                    ref[TILE_META * 8 + d : TILE_META * 8 + d + 1, :] = blocks[d][first : first + 1, :]
 
         def fill(ref, at, along, across):
             shift = (along, across) if colour == 0 else (across, along)
             owner = ((place[0] + shift[0]) % 4) * 4 + (place[1] + shift[1]) % 4
             for d in range(8):
                 rows = blocks[d][pl.ds(RIGHT_ROWS + colour * 32 + owner, 2, stride=16), :]
-                ref[at, d : d + 1, :] = rows[0:1]
-                ref[at + 1, d : d + 1, :] = rows[1:2]
+                ref[pl.ds(at * 8 + d, 2, stride=8), :] = rows
 
         for across in range(4):
             fill(up, size + 2 * across, 1, across)
@@ -345,7 +348,11 @@
 DOWN = [(i, (i - 1) % 4) for i in range(4)]
 
 
-def hop(axis, way, value):
+FAR_FIRST = (4, 6, 5, 7, 1, 3, 2)
+
+
+def hop(axis, way, *parts):
+    value = jnp.concatenate(parts, axis=0) if len(parts) > 1 else parts[0]
     return lax.ppermute(value, axis, way)
 
 
@@ -356,8 +363,8 @@
         state.append([up, own, hop(first, UP, up), hop(first, DOWN, down)])
     for (first, _), found, size in zip(axes, state, (65, 64)):
         a, b = found[2], found[3]
-        found.append(hop(first, UP, jnp.concatenate([a[:HALF], a[size + 8 :]], axis=0)))
-        found.append(hop(first, DOWN, jnp.concatenate([b[HALF:size], b[size + 8 :]], axis=0)))
+        found.append(hop(first, UP, a[:HALF], a[size + 8 :]))
+        found.append(hop(first, DOWN, b[HALF:size], b[size + 8 :]))
     for (_, second), found, size in zip(axes, state, (65, 64)):
         line = jnp.concatenate([found[0][:size], found[2][:size], found[3][:size]], axis=0)
         found.append(hop(second, UP, line))
@@ -368,13 +375,13 @@
         opposite = [c[:HALF], d[: n - HALF]]
         up = [own[2:4], a[n + 2 : n + 4], b[n + 2 : n + 4], c[HALF + 2 : HALF + 4], own[4:6], a[n + 4 : n + 6]]
         down = [own[6:8], a[n + 6 : n + 8], b[n + 6 : n + 8], d[n - HALF + 2 :], b[n + 4 : n + 6], d[n - HALF : n - HALF + 2]]
-        found.append(hop(second, UP, jnp.concatenate(opposite + up, axis=0)))
-        found.append(hop(second, DOWN, jnp.concatenate(opposite + down, axis=0)))
+        found.append(hop(second, UP, *opposite, *up))
+        found.append(hop(second, DOWN, *opposite, *down))
     for (_, second), found, n in zip(axes, state, (65, 64)):
         e, f, g, h = found[6:10]
         cut = n + HALF
-        found.append(hop(second, UP, jnp.concatenate([e[:cut], g[:HALF], g[n + 8 :]], axis=0)))
-        found.append(hop(second, DOWN, jnp.concatenate([f[cut:], h[HALF:n], h[n + 8 :]], axis=0)))
+        found.append(hop(second, UP, e[:cut], g[:HALF], g[n + 8 :]))
+        found.append(hop(second, DOWN, f[cut:], h[HALF:n], h[n + 8 :]))
     return state
 
 
@@ -395,19 +402,21 @@
             pltpu.VMEM((Q * 32, 128), F32),
             pltpu.SemaphoreType.DMA,
         ],
-        compiler_params=pltpu.CompilerParams(vmem_limit_bytes=56 * MIB),
+        compiler_params=pltpu.CompilerParams(vmem_limit_bytes=61 * MIB),
         name="measure",
     )(touched, spins, accept, site_ids, time_ids, left_proj, right_proj, weights, routing, perturb)
-    here = [blocks[0]] + [
-        lax.ppermute(blocks[d], ("zh", "c", "zl"), [(i, i ^ d) for i in range(8)]) for d in range(1, 8)
-    ]
+    here = [blocks[0]] + [None] * 7
+    for d in FAR_FIRST:
+        here[d] = lax.ppermute(blocks[d], ("zh", "c", "zl"), [(i, i ^ d) for i in range(8)])
     packed = pl.pallas_call(
         assemble_kernel,
-        out_shape=[sds(77, 8, 128), sds(77, 8, 128), sds(8, 8, 128), sds(76, 8, 128), sds(76, 8, 128), sds(8, 8, 128)],
+        out_shape=[sds(tiles * 8, 128) for tiles in (77, 77, 8, 76, 76, 8)],
         in_specs=[VMEM] * 8,
         out_specs=[VMEM] * 6,
+        compiler_params=pltpu.CompilerParams(vmem_limit_bytes=4 * MIB),
         name="assemble",
     )(*here)
+    packed = [rows.reshape(-1, 8, 128) for rows in packed]
     one, two = gather_planes((packed[:3], packed[3:]))
     return pl.pallas_call(
         final_kernel,

time: 131 us -> 128 us (0.977)
  waiting for transfers between devices: 65.8 us -> 70.2 us
  starting transfers between devices: 34.5 us -> 31.7 us
  Pallas kernels: 24.9 us -> 22.2 us
  local copies, waits for them, and re-layouts: 3.07 us -> 1.38 us
    ppermute x20, waiting for transfers between devices: 58.4 us -> 62.7 us  [hop(): return lax.ppermute(value, axis, way)]
    ppermute x20, starting transfers between devices: 24.1 us -> 21.3 us  [hop(): return lax.ppermute(value, axis, way)]
    pallas_call x1, Pallas kernels: 3.02 us -> 0.43 us  [per_device(): pl.pallas_call(assemble_kernel, out_shape=[sds(tiles * 8, 128) for tiles...]
    slice x2, local copies, waits for them, and re-layouts: 1.97 us -> 0.04 us  [gather_planes(): found[0][:size]]
  transfers between devices with their start and end apart: 27 -> 27, of which waited for: 13 -> 13; matrix products, arithmetic and copies ran while one was open for 2% -> 1% of each run, Pallas kernels for 0% -> 0%
where the time goes in v3:
time: 128 us
  waiting for transfers between devices  70.2 us (55%)
  starting transfers between devices  31.7 us (25%)
  Pallas kernels  22.2 us (17%)
  between operations  2 us (2%)
  local copies, waits for them, and re-layouts  1.38 us (1%)
    ppermute x20, waiting for transfers between devices, hop(): return lax.ppermute(value, axis, way)  62.7 us
    ppermute x20, starting transfers between devices, hop(): return lax.ppermute(value, axis, way)  21.3 us
    pallas_call x1, Pallas kernels, per_device(): pl.pallas_call(measure_kernel, out_shape=[sds(BLOCK_ROWS, 128)] * 8, in_s...  12 us
    ppermute x7, starting transfers between devices, per_device(): lax.ppermute(blocks[d], ('zh', 'c', 'zl'), [(i, i ^ d) for i in range(8)])  10.4 us
    pallas_call x1, Pallas kernels, per_device(): pl.pallas_call(final_kernel, out_shape=sds(GQ, 128, SITES * LEG), in_spec...  9.77 us
    ppermute x7, waiting for transfers between devices, per_device(): lax.ppermute(blocks[d], ('zh', 'c', 'zl'), [(i, i ^ d) for i in range(8)])  7.47 us
  transfers between devices with their start and end apart: 27, of which 13 were waited for; matrix products, arithmetic and copies ran while one was open for 1% of the time, Pallas kernels for 0%

profile of v3, /device:TPU:0, one launch (start us, length us, event | category | flops | bytes accessed | tf_op | source)
XLA Modules:
  0.0 127.8 jit_solution(10914403670608811455)
XLA Ops:
  1.3 12.0 %measure.1 = (f32[200,128]{1,0:T(8,128)}, f32[200,128]{1,0:T(8,128)}, f32[200,128]{1,0:T(8,128)}, f32[200,128]{1,0:T(8,128)}, f32[200,128]{1,0:T(8,128)}, /*inde...) custom-call(s32[1,4,64]{2,1,0:T(4,128)} %chosen_ref.1, s32[1,4,64]{2,1,0:T(4,128)} %spin_ref.1, ...), custom_call_target="tpu_custom_call" | custom-call | tf_op jit(solution)/shard_map/measure/pallas_call | solution.py:389
  13.3 2.1 %collective-permute-start = (f32[200,128]{1,0:T(8,128)}, f32[200,128]{1,0:T(8,128)S(1)}, u32[]{:S(2)}, u32[]{:S(2)}) collective-permute-start(f32[200,128]{1,0:T(8,128)} %get-tuple-element.20), channel_id=1, source_target_pairs={{0,1},{1,0},{32,33},{33,32},{64,65},{65,64},{96,97},{97,96},{2,3},... | collective-permute-start | bytes 307208 | tf_op jit(solution)/shard_map/ppermute | solution.py:410
  15.4 0.0 collective-permute-start.1
  15.4 0.2 collective-permute-start.2
  15.6 3.9 %collective-permute-start.3 = (f32[200,128]{1,0:T(8,128)}, f32[200,128]{1,0:T(8,128)S(1)}, u32[]{:S(2)}, u32[]{:S(2)}) collective-permute-start(f32[200,128]{1,0:T(8,128)} %get-tuple-element.23), channel_id=1, source_target_pairs={{0,64},{1,65},{32,96},{33,97},{64,0},{65,1},{96,32},{97,33},{2,66}... | collective-permute-start | bytes 307208 | tf_op jit(solution)/shard_map/ppermute | solution.py:410
  19.5 0.7 collective-permute-start.4
  20.3 0.0 collective-permute-done.refs_1_
  20.3 1.4 %collective-permute-start.5 = (f32[200,128]{1,0:T(8,128)}, f32[200,128]{1,0:T(8,128)S(1)}, u32[]{:S(2)}, u32[]{:S(2)}) collective-permute-start(f32[200,128]{1,0:T(8,128)} %get-tuple-element.25), channel_id=1, source_target_pairs={{0,96},{1,97},{32,64},{33,65},{64,32},{65,33},{96,0},{97,1},{2,98}... | collective-permute-start | bytes 307208 | tf_op jit(solution)/shard_map/ppermute | solution.py:410
  21.7 0.0 collective-permute-done.1.refs_2_
  21.7 2.1 %collective-permute-start.6 = (f32[200,128]{1,0:T(8,128)}, f32[200,128]{1,0:T(8,128)S(1)}, u32[]{:S(2)}, u32[]{:S(2)}) collective-permute-start(f32[200,128]{1,0:T(8,128)} %get-tuple-element.26), channel_id=1, source_target_pairs={{0,97},{1,96},{32,65},{33,64},{64,33},{65,32},{96,1},{97,0},{2,99}... | collective-permute-start | bytes 307208 | tf_op jit(solution)/shard_map/ppermute | solution.py:410
  23.8 0.0 collective-permute-done.2.refs_3_
  23.8 3.6 %collective-permute-done.3.refs_4_ = f32[200,128]{1,0:T(8,128)S(1)} collective-permute-done((f32[200,128]{1,0:T(8,128)}, f32[200,128]{1,0:T(8,128)S(1)}, u32[]{:S(2)}, u32[]{:S(2)}) %collective-permute-start.3) | collective-permute-done | bytes 102432 | tf_op jit(solution)/shard_map/ppermute | solution.py:410
  27.4 2.9 %collective-permute-done.4.refs_5_ = f32[200,128]{1,0:T(8,128)S(1)} collective-permute-done((f32[200,128]{1,0:T(8,128)}, f32[200,128]{1,0:T(8,128)S(1)}, u32[]{:S(2)}, u32[]{:S(2)}) %collective-permute-start.4) | collective-permute-done | bytes 102432 | tf_op jit(solution)/shard_map/ppermute | solution.py:410
  30.3 0.0 collective-permute-done.5.refs_6_
  30.3 0.9 collective-permute-done.6.refs_7_
  31.2 0.9 copy-done
  32.1 0.4 assemble.1
  32.6 3.1 %collective-permute-start.18 = (f32[76,8,128]{2,1,0:T(8,128)S(1)}, f32[76,8,128]{2,1,0:T(8,128)S(1)}, u32[]{:S(2)}, u32[]{:S(2)}) collective-permute-start(f32[76,8,128]{2,1,0:T(8,128)S(1)} %bitcast.31), channel_id=1, source_target_pairs={{0,6},{2,0},{4,2},{6,4},{1,7},{3,1},{5,3},{7,5},{8,14},{10,8},{12,... | collective-permute-start | bytes 933896 | tf_op jit(solution)/shard_map/ppermute | solution.py:356
  35.7 0.0 collective-permute-start.17
  35.7 2.8 %collective-permute-start.8 = (f32[77,8,128]{2,1,0:T(8,128)S(1)}, f32[77,8,128]{2,1,0:T(8,128)S(1)}, u32[]{:S(2)}, u32[]{:S(2)}) collective-permute-start(f32[77,8,128]{2,1,0:T(8,128)S(1)} %bitcast.30), channel_id=1, source_target_pairs={{0,24},{8,0},{16,8},{24,16},{1,25},{9,1},{17,9},{25,17},{2,26},{10... | collective-permute-start | bytes 946184 | tf_op jit(solution)/shard_map/ppermute | solution.py:356
  38.5 0.0 collective-permute-start.7
  38.5 4.3 %collective-permute-done.18.refs_15_ = f32[76,8,128]{2,1,0:T(8,128)S(1)} collective-permute-done((f32[76,8,128]{2,1,0:T(8,128)S(1)}, f32[76,8,128]{2,1,0:T(8,128)S(1)}, u32[]{:S(2)}, u32[]{:S(2)}) %collective-permute-start.18) | collective-permute-done | bytes 311328 | tf_op jit(solution)/shard_map/ppermute | solution.py:356
  42.9 3.4 %collective-permute-done.17.refs_14_ = f32[76,8,128]{2,1,0:T(8,128)S(1)} collective-permute-done((f32[76,8,128]{2,1,0:T(8,128)S(1)}, f32[76,8,128]{2,1,0:T(8,128)S(1)}, u32[]{:S(2)}, u32[]{:S(2)}) %collective-permute-start.17) | collective-permute-done | bytes 311328 | tf_op jit(solution)/shard_map/ppermute | solution.py:356
  46.3 0.1 pad_maximum_fusion.1
  46.4 0.0 slice-start
  46.4 2.8 %collective-permute-start.22 = (f32[192,8,128]{2,1,0:T(8,128)S(1)}, f32[192,8,128]{2,1,0:T(8,128)S(1)}, u32[]{:S(2)}, u32[]{:S(2)}) collective-permute-start(f32[192,8,128]{2,1,0:T(8,128)S(1)} %pad_maximum_fusion.1), channel_id=1, source_target_pairs={{0,24},{8,0},{16,8},{24,16},{1,25},{9,1},{17,9},{25,17},{2,26},{10... | collective-permute-start | bytes 2359304 | tf_op jit(solution)/shard_map/ppermute | solution.py:356
  49.2 0.0 collective-permute-start.21
  49.3 0.6 collective-permute-start.20
  49.9 0.0 collective-permute-done.8.refs_3_
  49.9 1.8 %collective-permute-start.19 = (f32[36,8,128]{2,1,0:T(8,128)S(1)}, f32[36,8,128]{2,1,0:T(8,128)S(1)}, u32[]{:S(2)}, u32[]{:S(2)}) collective-permute-start(f32[36,8,128]{2,1,0:T(8,128)S(1)} %pad_maximum_fusion.8), channel_id=1, source_target_pairs={{0,2},{2,4},{4,6},{6,0},{1,3},{3,5},{5,7},{7,1},{8,10},{10,12},{12... | collective-permute-start | bytes 442376 | tf_op jit(solution)/shard_map/ppermute | solution.py:356
  51.7 0.0 collective-permute-done.7.refs_2_
  51.7 3.3 %collective-permute-start.10 = (f32[37,8,128]{2,1,0:T(8,128)S(1)}, f32[37,8,128]{2,1,0:T(8,128)S(1)}, u32[]{:S(2)}, u32[]{:S(2)}) collective-permute-start(f32[37,8,128]{2,1,0:T(8,128)S(1)} %pad_maximum_fusion.6), channel_id=1, source_target_pairs={{0,24},{8,0},{16,8},{24,16},{1,25},{9,1},{17,9},{25,17},{2,26},{10... | collective-permute-start | bytes 454664 | tf_op jit(solution)/shard_map/ppermute | solution.py:356
  55.1 0.1 pad_maximum_fusion
  55.2 1.1 collective-permute-done.19.refs_16_
  56.3 0.8 collective-permute-start.9
  57.1 0.0 collective-permute-done.20.refs_17_
  57.1 0.1 collective-permute-start.12
  57.3 14.8 %collective-permute-done.9.refs_4_ = f32[36,8,128]{2,1,0:T(8,128)S(1)} collective-permute-done((f32[36,8,128]{2,1,0:T(8,128)S(1)}, f32[36,8,128]{2,1,0:T(8,128)S(1)}, u32[]{:S(2)}, u32[]{:S(2)}) %collective-permute-start.9) | collective-permute-done | bytes 147488 | tf_op jit(solution)/shard_map/ppermute | solution.py:356
  72.1 0.0 collective-permute-start.23
  72.1 0.0 collective-permute-done.10.refs_5_
  72.1 3.3 %collective-permute-start.24 = (f32[76,8,128]{2,1,0:T(8,128)S(1)}, f32[76,8,128]{2,1,0:T(8,128)S(1)}, u32[]{:S(2)}, u32[]{:S(2)}) collective-permute-start(f32[76,8,128]{2,1,0:T(8,128)S(1)} %constant_dynamic-update-slice_fusion.18), channel_id=1, source_target_pairs={{0,24},{8,0},{16,8},{24,16},{1,25},{9,1},{17,9},{25,17},{2,26},{10... | collective-permute-start | bytes 933896 | tf_op jit(solution)/shard_map/ppermute | solution.py:356
  75.5 5.2 %collective-permute-done.23.refs_20_ = f32[76,8,128]{2,1,0:T(8,128)S(1)} collective-permute-done((f32[76,8,128]{2,1,0:T(8,128)S(1)}, f32[76,8,128]{2,1,0:T(8,128)S(1)}, u32[]{:S(2)}, u32[]{:S(2)}) %collective-permute-start.23) | collective-permute-done | bytes 311328 | tf_op jit(solution)/shard_map/ppermute | solution.py:356
  80.7 0.0 collective-permute-start.13
  80.7 0.0 collective-permute-done.24.refs_21_
  80.7 0.0 collective-permute-start.11
  80.7 11.5 %collective-permute-done.13.refs_8_ = f32[77,8,128]{2,1,0:T(8,128)S(1)} collective-permute-done((f32[77,8,128]{2,1,0:T(8,128)S(1)}, f32[77,8,128]{2,1,0:T(8,128)S(1)}, u32[]{:S(2)}, u32[]{:S(2)}) %collective-permute-start.13) | collective-permute-done | bytes 315424 | tf_op jit(solution)/shard_map/ppermute | solution.py:356
  92.2 0.0 collective-permute-start.14
  92.3 0.0 slice-start.1
  92.3 10.2 %collective-permute-done.14.refs_9_ = f32[77,8,128]{2,1,0:T(8,128)S(1)} collective-permute-done((f32[77,8,128]{2,1,0:T(8,128)S(1)}, f32[77,8,128]{2,1,0:T(8,128)S(1)}, u32[]{:S(2)}, u32[]{:S(2)}) %collective-permute-start.14) | collective-permute-done | bytes 315424 | tf_op jit(solution)/shard_map/ppermute | solution.py:356
  102.6 0.0 collective-permute-done.22.refs_19_
  102.7 0.1 collective-permute-start.26
  102.8 0.0 collective-permute-done.21.refs_18_
  102.8 0.0 collective-permute-done.12.refs_7_
  102.9 1.3 %collective-permute-start.16 = (f32[135,8,128]{2,1,0:T(8,128)S(1)}, f32[135,8,128]{2,1,0:T(8,128)S(1)}, u32[]{:S(2)}, u32[]{:S(2)}) collective-permute-start(f32[135,8,128]{2,1,0:T(8,128)S(1)} %pad_maximum_fusion.2), channel_id=1, source_target_pairs={{0,6},{2,0},{4,2},{6,4},{1,7},{3,1},{5,3},{7,5},{8,14},{10,8},{12,... | collective-permute-start | bytes 1658888 | tf_op jit(solution)/shard_map/ppermute | solution.py:356
  104.2 1.5 %collective-permute-done.11.refs_6_ = f32[195,8,128]{2,1,0:T(8,128)S(1)} collective-permute-done((f32[195,8,128]{2,1,0:T(8,128)S(1)}, f32[195,8,128]{2,1,0:T(8,128)S(1)}, u32[]{:S(2)}, u32[]{:S(2)}) %collective-permute-start.11) | collective-permute-done | bytes 798752 | tf_op jit(solution)/shard_map/ppermute | solution.py:356
  105.8 0.1 collective-permute-start.15
  105.9 1.3 %collective-permute-start.25 = (f32[132,8,128]{2,1,0:T(8,128)S(1)}, f32[132,8,128]{2,1,0:T(8,128)S(1)}, u32[]{:S(2)}, u32[]{:S(2)}) collective-permute-start(f32[132,8,128]{2,1,0:T(8,128)S(1)} %pad_maximum_fusion.4), channel_id=1, source_target_pairs={{0,8},{8,16},{16,24},{24,0},{1,9},{9,17},{17,25},{25,1},{2,10},{10... | collective-permute-start | bytes 1622024 | tf_op jit(solution)/shard_map/ppermute | solution.py:356
  107.2 4.9 %collective-permute-done.26.refs_23_ = f32[132,8,128]{2,1,0:T(8,128)S(1)} collective-permute-done((f32[132,8,128]{2,1,0:T(8,128)S(1)}, f32[132,8,128]{2,1,0:T(8,128)S(1)}, u32[]{:S(2)}, u32[]{:S(2)}) %collective-permute-start.26) | collective-permute-done | bytes 540704 | tf_op jit(solution)/shard_map/ppermute | solution.py:356
  112.1 5.7 %collective-permute-done.25.refs_22_ = f32[132,8,128]{2,1,0:T(8,128)S(1)} collective-permute-done((f32[132,8,128]{2,1,0:T(8,128)S(1)}, f32[132,8,128]{2,1,0:T(8,128)S(1)}, u32[]{:S(2)}, u32[]{:S(2)}) %collective-permute-start.25) | collective-permute-done | bytes 540704 | tf_op jit(solution)/shard_map/ppermute | solution.py:356
  117.8 0.0 collective-permute-done.15.refs_10_
  117.8 0.0 collective-permute-done.16.refs_11_
  117.8 0.0 slice-done
  117.8 0.0 slice-done.1
  117.9 9.8 %accumulate.1 = f32[4,128,4096]{2,1,0:T(8,128)} custom-call(f32[77,8,128]{2,1,0:T(8,128)S(1)} %bitcast.25, f32[8,8,128]{2,1,0:T(8,128)S(1)} %bitcast.28, f32[77,8,128]{2,1,0:T(8,128)S(1)} %collective-permute-done.7.refs_2_, f32[77,8,128]{2,1,0:T(8,128)S(1)} %collective-permute-done.8.refs_3_, f32[36,8,128]{2,1,0:T(8,128)S(1)} %collective-permute-done.9.refs_4_, ...), custom_call_target="tpu_custom_call" | custom-call | tf_op jit(solution)/shard_map/accumulate/pallas_call | solution.py:421
  (62 shorter events, 0.7 us)
Async XLA Ops:
  13.3 6.9 %collective-permute-start = (f32[200,128]{1,0:T(8,128)}, f32[200,128]{1,0:T(8,128)S(1)}, u32[]{:S(2)}, u32[]{:S(2)}) collective-permute-start(f32[200,128]{1,0:T(8,128)} %get-tuple-element.20), channel_id=1, source_target_pairs={{0,1},{1,0},{32,33},{33,32},{64,65},{65,64},{96,97},{97,96},{2,3},... | collective-permute-start | bytes 307208 | tf_op jit(solution)/shard_map/ppermute | solution.py:410
  15.4 6.2 %collective-permute-start.1 = (f32[200,128]{1,0:T(8,128)}, f32[200,128]{1,0:T(8,128)S(1)}, u32[]{:S(2)}, u32[]{:S(2)}) collective-permute-start(f32[200,128]{1,0:T(8,128)} %get-tuple-element.21), channel_id=1, source_target_pairs={{0,32},{1,33},{32,0},{33,1},{64,96},{65,97},{96,64},{97,65},{2,34}... | collective-permute-start | bytes 307208 | tf_op jit(solution)/shard_map/ppermute | solution.py:410
  15.4 8.3 %collective-permute-start.2 = (f32[200,128]{1,0:T(8,128)}, f32[200,128]{1,0:T(8,128)S(1)}, u32[]{:S(2)}, u32[]{:S(2)}) collective-permute-start(f32[200,128]{1,0:T(8,128)} %get-tuple-element.22), channel_id=1, source_target_pairs={{0,33},{1,32},{32,1},{33,0},{64,97},{65,96},{96,65},{97,64},{2,35}... | collective-permute-start | bytes 307208 | tf_op jit(solution)/shard_map/ppermute | solution.py:410
  15.6 11.8 %collective-permute-start.3 = (f32[200,128]{1,0:T(8,128)}, f32[200,128]{1,0:T(8,128)S(1)}, u32[]{:S(2)}, u32[]{:S(2)}) collective-permute-start(f32[200,128]{1,0:T(8,128)} %get-tuple-element.23), channel_id=1, source_target_pairs={{0,64},{1,65},{32,96},{33,97},{64,0},{65,1},{96,32},{97,33},{2,66}... | collective-permute-start | bytes 307208 | tf_op jit(solution)/shard_map/ppermute | solution.py:410
  19.5 10.7 %collective-permute-start.4 = (f32[200,128]{1,0:T(8,128)}, f32[200,128]{1,0:T(8,128)S(1)}, u32[]{:S(2)}, u32[]{:S(2)}) collective-permute-start(f32[200,128]{1,0:T(8,128)} %get-tuple-element.24), channel_id=1, source_target_pairs={{0,65},{1,64},{32,97},{33,96},{64,1},{65,0},{96,33},{97,32},{2,67}... | collective-permute-start | bytes 307208 | tf_op jit(solution)/shard_map/ppermute | solution.py:410
  20.3 10.0 %collective-permute-start.5 = (f32[200,128]{1,0:T(8,128)}, f32[200,128]{1,0:T(8,128)S(1)}, u32[]{:S(2)}, u32[]{:S(2)}) collective-permute-start(f32[200,128]{1,0:T(8,128)} %get-tuple-element.25), channel_id=1, source_target_pairs={{0,96},{1,97},{32,64},{33,65},{64,32},{65,33},{96,0},{97,1},{2,98}... | collective-permute-start | bytes 307208 | tf_op jit(solution)/shard_map/ppermute | solution.py:410
  21.7 9.6 %collective-permute-start.6 = (f32[200,128]{1,0:T(8,128)}, f32[200,128]{1,0:T(8,128)S(1)}, u32[]{:S(2)}, u32[]{:S(2)}) collective-permute-start(f32[200,128]{1,0:T(8,128)} %get-tuple-element.26), channel_id=1, source_target_pairs={{0,97},{1,96},{32,65},{33,64},{64,33},{65,32},{96,1},{97,0},{2,99}... | collective-permute-start | bytes 307208 | tf_op jit(solution)/shard_map/ppermute | solution.py:410
  31.2 0.9 copy-start
  32.6 10.3 %collective-permute-start.18 = (f32[76,8,128]{2,1,0:T(8,128)S(1)}, f32[76,8,128]{2,1,0:T(8,128)S(1)}, u32[]{:S(2)}, u32[]{:S(2)}) collective-permute-start(f32[76,8,128]{2,1,0:T(8,128)S(1)} %bitcast.31), channel_id=1, source_target_pairs={{0,6},{2,0},{4,2},{6,4},{1,7},{3,1},{5,3},{7,5},{8,14},{10,8},{12,... | collective-permute-start | bytes 933896 | tf_op jit(solution)/shard_map/ppermute | solution.py:356
  35.7 10.6 %collective-permute-start.17 = (f32[76,8,128]{2,1,0:T(8,128)S(1)}, f32[76,8,128]{2,1,0:T(8,128)S(1)}, u32[]{:S(2)}, u32[]{:S(2)}) collective-permute-start(f32[76,8,128]{2,1,0:T(8,128)S(1)} %bitcast.26), channel_id=1, source_target_pairs={{0,2},{2,4},{4,6},{6,0},{1,3},{3,5},{5,7},{7,1},{8,10},{10,12},{12... | collective-permute-start | bytes 933896 | tf_op jit(solution)/shard_map/ppermute | solution.py:356
  35.7 14.2 %collective-permute-start.8 = (f32[77,8,128]{2,1,0:T(8,128)S(1)}, f32[77,8,128]{2,1,0:T(8,128)S(1)}, u32[]{:S(2)}, u32[]{:S(2)}) collective-permute-start(f32[77,8,128]{2,1,0:T(8,128)S(1)} %bitcast.30), channel_id=1, source_target_pairs={{0,24},{8,0},{16,8},{24,16},{1,25},{9,1},{17,9},{25,17},{2,26},{10... | collective-permute-start | bytes 946184 | tf_op jit(solution)/shard_map/ppermute | solution.py:356
  38.5 13.2 %collective-permute-start.7 = (f32[77,8,128]{2,1,0:T(8,128)S(1)}, f32[77,8,128]{2,1,0:T(8,128)S(1)}, u32[]{:S(2)}, u32[]{:S(2)}) collective-permute-start(f32[77,8,128]{2,1,0:T(8,128)S(1)} %bitcast.24), channel_id=1, source_target_pairs={{0,8},{8,16},{16,24},{24,0},{1,9},{9,17},{17,25},{25,1},{2,10},{10... | collective-permute-start | bytes 946184 | tf_op jit(solution)/shard_map/ppermute | solution.py:356
  46.4 71.5 %slice-start = ((s8[8388608]{0:T(1024)(128)(4,1)}), s8[4194304]{0:T(1024)(128)(4,1)S(1)}, s32[]{:S(2)}) async-start(s8[8388608]{0:T(1024)(128)(4,1)} %bitcast.22), calls=%async_computation | async-start | bytes 8388608
  46.4 56.2 %collective-permute-start.22 = (f32[192,8,128]{2,1,0:T(8,128)S(1)}, f32[192,8,128]{2,1,0:T(8,128)S(1)}, u32[]{:S(2)}, u32[]{:S(2)}) collective-permute-start(f32[192,8,128]{2,1,0:T(8,128)S(1)} %pad_maximum_fusion.1), channel_id=1, source_target_pairs={{0,24},{8,0},{16,8},{24,16},{1,25},{9,1},{17,9},{25,17},{2,26},{10... | collective-permute-start | bytes 2359304 | tf_op jit(solution)/shard_map/ppermute | solution.py:356
  49.2 53.5 %collective-permute-start.21 = (f32[192,8,128]{2,1,0:T(8,128)S(1)}, f32[192,8,128]{2,1,0:T(8,128)S(1)}, u32[]{:S(2)}, u32[]{:S(2)}) collective-permute-start(f32[192,8,128]{2,1,0:T(8,128)S(1)} %pad_maximum_fusion.1), channel_id=1, source_target_pairs={{0,8},{8,16},{16,24},{24,0},{1,9},{9,17},{17,25},{25,1},{2,10},{10... | collective-permute-start | bytes 2359304 | tf_op jit(solution)/shard_map/ppermute | solution.py:356
  49.3 7.8 %collective-permute-start.20 = (f32[36,8,128]{2,1,0:T(8,128)S(1)}, f32[36,8,128]{2,1,0:T(8,128)S(1)}, u32[]{:S(2)}, u32[]{:S(2)}) collective-permute-start(f32[36,8,128]{2,1,0:T(8,128)S(1)} %pad_maximum_fusion.9), channel_id=1, source_target_pairs={{0,6},{2,0},{4,2},{6,4},{1,7},{3,1},{5,3},{7,5},{8,14},{10,8},{12,... | collective-permute-start | bytes 442376 | tf_op jit(solution)/shard_map/ppermute | solution.py:356
  49.9 6.4 %collective-permute-start.19 = (f32[36,8,128]{2,1,0:T(8,128)S(1)}, f32[36,8,128]{2,1,0:T(8,128)S(1)}, u32[]{:S(2)}, u32[]{:S(2)}) collective-permute-start(f32[36,8,128]{2,1,0:T(8,128)S(1)} %pad_maximum_fusion.8), channel_id=1, source_target_pairs={{0,2},{2,4},{4,6},{6,0},{1,3},{3,5},{5,7},{7,1},{8,10},{10,12},{12... | collective-permute-start | bytes 442376 | tf_op jit(solution)/shard_map/ppermute | solution.py:356
  51.7 20.4 %collective-permute-start.10 = (f32[37,8,128]{2,1,0:T(8,128)S(1)}, f32[37,8,128]{2,1,0:T(8,128)S(1)}, u32[]{:S(2)}, u32[]{:S(2)}) collective-permute-start(f32[37,8,128]{2,1,0:T(8,128)S(1)} %pad_maximum_fusion.6), channel_id=1, source_target_pairs={{0,24},{8,0},{16,8},{24,16},{1,25},{9,1},{17,9},{25,17},{2,26},{10... | collective-permute-start | bytes 454664 | tf_op jit(solution)/shard_map/ppermute | solution.py:356
  56.3 15.8 %collective-permute-start.9 = (f32[36,8,128]{2,1,0:T(8,128)S(1)}, f32[36,8,128]{2,1,0:T(8,128)S(1)}, u32[]{:S(2)}, u32[]{:S(2)}) collective-permute-start(f32[36,8,128]{2,1,0:T(8,128)S(1)} %pad_maximum_fusion.7), channel_id=1, source_target_pairs={{0,8},{8,16},{16,24},{24,0},{1,9},{9,17},{17,25},{25,1},{2,10},{10... | collective-permute-start | bytes 442376 | tf_op jit(solution)/shard_map/ppermute | solution.py:356
  57.1 45.7 %collective-permute-start.12 = (f32[195,8,128]{2,1,0:T(8,128)S(1)}, f32[195,8,128]{2,1,0:T(8,128)S(1)}, u32[]{:S(2)}, u32[]{:S(2)}) collective-permute-start(f32[195,8,128]{2,1,0:T(8,128)S(1)} %pad_maximum_fusion), channel_id=1, source_target_pairs={{0,6},{2,0},{4,2},{6,4},{1,7},{3,1},{5,3},{7,5},{8,14},{10,8},{12,... | collective-permute-start | bytes 2396168 | tf_op jit(solution)/shard_map/ppermute | solution.py:356
  72.1 8.6 %collective-permute-start.23 = (f32[76,8,128]{2,1,0:T(8,128)S(1)}, f32[76,8,128]{2,1,0:T(8,128)S(1)}, u32[]{:S(2)}, u32[]{:S(2)}) collective-permute-start(f32[76,8,128]{2,1,0:T(8,128)S(1)} %constant_dynamic-update-slice_fusion.12), channel_id=1, source_target_pairs={{0,8},{8,16},{16,24},{24,0},{1,9},{9,17},{17,25},{25,1},{2,10},{10... | collective-permute-start | bytes 933896 | tf_op jit(solution)/shard_map/ppermute | solution.py:356
  72.1 8.6 %collective-permute-start.24 = (f32[76,8,128]{2,1,0:T(8,128)S(1)}, f32[76,8,128]{2,1,0:T(8,128)S(1)}, u32[]{:S(2)}, u32[]{:S(2)}) collective-permute-start(f32[76,8,128]{2,1,0:T(8,128)S(1)} %constant_dynamic-update-slice_fusion.18), channel_id=1, source_target_pairs={{0,24},{8,0},{16,8},{24,16},{1,25},{9,1},{17,9},{25,17},{2,26},{10... | collective-permute-start | bytes 933896 | tf_op jit(solution)/shard_map/ppermute | solution.py:356
  80.7 11.5 %collective-permute-start.13 = (f32[77,8,128]{2,1,0:T(8,128)S(1)}, f32[77,8,128]{2,1,0:T(8,128)S(1)}, u32[]{:S(2)}, u32[]{:S(2)}) collective-permute-start(f32[77,8,128]{2,1,0:T(8,128)S(1)} %constant_dynamic-update-slice_fusion), channel_id=1, source_target_pairs={{0,2},{2,4},{4,6},{6,0},{1,3},{3,5},{5,7},{7,1},{8,10},{10,12},{12... | collective-permute-start | bytes 946184 | tf_op jit(solution)/shard_map/ppermute | solution.py:356
  80.7 25.0 %collective-permute-start.11 = (f32[195,8,128]{2,1,0:T(8,128)S(1)}, f32[195,8,128]{2,1,0:T(8,128)S(1)}, u32[]{:S(2)}, u32[]{:S(2)}) collective-permute-start(f32[195,8,128]{2,1,0:T(8,128)S(1)} %pad_maximum_fusion), channel_id=1, source_target_pairs={{0,2},{2,4},{4,6},{6,0},{1,3},{3,5},{5,7},{7,1},{8,10},{10,12},{12... | collective-permute-start | bytes 2396168 | tf_op jit(solution)/shard_map/ppermute | solution.py:356
  92.2 10.3 %collective-permute-start.14 = (f32[77,8,128]{2,1,0:T(8,128)S(1)}, f32[77,8,128]{2,1,0:T(8,128)S(1)}, u32[]{:S(2)}, u32[]{:S(2)}) collective-permute-start(f32[77,8,128]{2,1,0:T(8,128)S(1)} %constant_dynamic-update-slice_fusion.6), channel_id=1, source_target_pairs={{0,6},{2,0},{4,2},{6,4},{1,7},{3,1},{5,3},{7,5},{8,14},{10,8},{12,... | collective-permute-start | bytes 946184 | tf_op jit(solution)/shard_map/ppermute | solution.py:356
  92.3 25.6 %slice-start.1 = ((s8[8388608]{0:T(1024)(128)(4,1)}), s8[4194304]{0:T(1024)(128)(4,1)S(1)}, s32[]{:S(2)}) async-start(s8[8388608]{0:T(1024)(128)(4,1)} %bitcast.22), calls=%async_computation.1 | async-start | bytes 8388608
  102.7 9.4 %collective-permute-start.26 = (f32[132,8,128]{2,1,0:T(8,128)S(1)}, f32[132,8,128]{2,1,0:T(8,128)S(1)}, u32[]{:S(2)}, u32[]{:S(2)}) collective-permute-start(f32[132,8,128]{2,1,0:T(8,128)S(1)} %pad_maximum_fusion.5), channel_id=1, source_target_pairs={{0,24},{8,0},{16,8},{24,16},{1,25},{9,1},{17,9},{25,17},{2,26},{10... | collective-permute-start | bytes 1622024 | tf_op jit(solution)/shard_map/ppermute | solution.py:356
  102.9 14.9 %collective-permute-start.16 = (f32[135,8,128]{2,1,0:T(8,128)S(1)}, f32[135,8,128]{2,1,0:T(8,128)S(1)}, u32[]{:S(2)}, u32[]{:S(2)}) collective-permute-start(f32[135,8,128]{2,1,0:T(8,128)S(1)} %pad_maximum_fusion.2), channel_id=1, source_target_pairs={{0,6},{2,0},{4,2},{6,4},{1,7},{3,1},{5,3},{7,5},{8,14},{10,8},{12,... | collective-permute-start | bytes 1658888 | tf_op jit(solution)/shard_map/ppermute | solution.py:356
  105.8 12.1 %collective-permute-start.15 = (f32[133,8,128]{2,1,0:T(8,128)S(1)}, f32[133,8,128]{2,1,0:T(8,128)S(1)}, u32[]{:S(2)}, u32[]{:S(2)}) collective-permute-start(f32[133,8,128]{2,1,0:T(8,128)S(1)} %pad_maximum_fusion.3), channel_id=1, source_target_pairs={{0,2},{2,4},{4,6},{6,0},{1,3},{3,5},{5,7},{7,1},{8,10},{10,12},{12... | collective-permute-start | bytes 1634312 | tf_op jit(solution)/shard_map/ppermute | solution.py:356
  105.9 11.9 %collective-permute-start.25 = (f32[132,8,128]{2,1,0:T(8,128)S(1)}, f32[132,8,128]{2,1,0:T(8,128)S(1)}, u32[]{:S(2)}, u32[]{:S(2)}) collective-permute-start(f32[132,8,128]{2,1,0:T(8,128)S(1)} %pad_maximum_fusion.4), channel_id=1, source_target_pairs={{0,8},{8,16},{16,24},{24,0},{1,9},{9,17},{17,25},{25,1},{2,10},{10... | collective-permute-start | bytes 1622024 | tf_op jit(solution)/shard_map/ppermute | solution.py:356
